TPU v7x, 128 devices: a whole 4x4x4 slice. The times are simulated.
128 devices in a mesh: gx: 32 (over y, z, core), gy: 4 (over x).
Axes of the slice: x: 4, y: 4, z: 4, core: 2. Of those that a mesh axis runs over, the one named last changes fastest.
Arguments:
- right_side: float32 [3, 128, 64, 256], P(None, 'gx', 'gy'), may hold values from -45 to 45
- diag_blocks: float32 [9, 128, 64, 256], P(None, 'gx', 'gy'), may hold values from -1.2 to 1.8
- off_blocks: float32 [6, 9, 128, 64, 256], P(None, None, 'gx', 'gy'), may hold values from -0.25 to 0.16
- cell_inverse: float32 [9, 128, 64, 256], P(None, 'gx', 'gy'), may hold values from -0.4 to 0.85
- send_cells: int32 [128, 3200], P(('gx', 'gy')), may hold values from 0 to 16383, as said below
- recv_index: int32 [1024, 400], P(('gx', 'gy')), may hold values from 0 to 28799, as said below
- seg_count: int32 [1024], P(('gx', 'gy')), may hold values from 50 to 400, as said below
- span_inverse: float32 [25, 48, 49152], P(None, None, ('gx', 'gy')), may hold values from -0.24 to 1.2
- span_couple: float32 [25, 9, 1024], P(None, None, ('gx', 'gy')), may hold values from -3 to 3
Outputs:
- solution: float32 [3, 128, 64, 256], P(None, 'gx', 'gy')
- residual: float32 [3, 128, 64, 256], P(None, 'gx', 'gy')
Inputs may be any that keep to these rules, and one draw needn't show every extreme that they name: `send_cells`: each row holds distinct local cells of its device. `recv_index`: over the live segments of one owner's wells the positions are distinct and name tiles inside the grid; entries of segments that are not live are arbitrary. `seg_count`: on one device in every draw all wells have 400 segments.
All inputs are finite; a program needn't handle non-finite values.
Results may differ from a plain program's by a relative error of at most 0.0001.
Values sent between devices are 32-bit elements; how exact they have to be, the bound alone decides.
A program may use at most 128 MiB of HBM per device.

v0:
```python
import jax
import jax.numpy as jnp
from jax import lax
from jax.sharding import PartitionSpec as P

MAXSEG = 400
SPAN = 16
NCHUNK = 25


def with_halo(cells, sides, width):
    for axis, dim in sides:
        count = lax.axis_size(axis)
        ends = count - 1
        head = lax.slice_in_dim(cells, 0, width, axis=dim)
        tail = lax.slice_in_dim(cells, cells.shape[dim] - width, cells.shape[dim], axis=dim)
        cells = jnp.concatenate(
            [
                lax.ppermute(tail, axis, [(i, (i + 1) % count) for i in range(ends)]),
                cells,
                lax.ppermute(head, axis, [((i + 1) % count, i) for i in range(ends)]),
            ],
            axis=dim,
        )
    return cells


def block_apply(matrix, vector):
    return jnp.stack(
        [
            matrix[3 * a] * vector[0]
            + matrix[3 * a + 1] * vector[1]
            + matrix[3 * a + 2] * vector[2]
            for a in range(3)
        ]
    )


def apply_jacobian(field, diag_blocks, off_blocks):
    padded = with_halo(field, (("gx", 1), ("gy", 2)), 1)
    padded = jnp.pad(padded, ((0, 0), (0, 0), (0, 0), (1, 1)))
    beside = [
        padded[:, :-2, 1:-1, 1:-1],
        padded[:, 2:, 1:-1, 1:-1],
        padded[:, 1:-1, :-2, 1:-1],
        padded[:, 1:-1, 2:, 1:-1],
        padded[:, 1:-1, 1:-1, :-2],
        padded[:, 1:-1, 1:-1, 2:],
    ]
    total = block_apply(diag_blocks, field)
    for face in range(6):
        total = total + block_apply(off_blocks[face], beside[face])
    return total


def chain_solve(segments, span_inverse, span_couple):
    well_count = span_couple.shape[2]
    width = 3 * SPAN
    blocks = (
        segments.reshape(3, well_count, NCHUNK, SPAN)
        .transpose(2, 3, 0, 1)
        .reshape(NCHUNK, width, well_count)
    )
    inverse = span_inverse.reshape(NCHUNK, width, well_count, width)

    def advance(carry, packed):
        block_rhs, block_inverse, couple = packed
        first = block_rhs[:3] - block_apply(couple, carry)
        block_rhs = jnp.concatenate([first, block_rhs[3:]], axis=0)
        solved = jnp.sum(block_inverse * block_rhs[:, :, None], axis=0).T
        return (solved[width - 3 :], solved)

    start = jnp.zeros((3, well_count), jnp.float32)
    _, solved = lax.scan(advance, start, (blocks, inverse, span_couple))
    return (
        solved.reshape(NCHUNK, SPAN, 3, well_count)
        .transpose(2, 3, 0, 1)
        .reshape(3, well_count * MAXSEG)
    )


def gather_blocks(perforated):
    count = perforated.shape[0]
    beside_all = with_halo(perforated.reshape(count, 1, 1, -1), (("gx", 1), ("gy", 2)), 1)
    return beside_all.reshape(count, -1)


def gather_values(picked):
    count = picked.shape[0]
    beside_all = with_halo(picked.reshape(count, 1, 1, -1), (("gx", 1), ("gy", 2)), 1)
    return beside_all.reshape(count, -1)


def return_values(slots):
    count = slots.shape[0]
    spread = with_halo(slots.reshape(count, 3, 3, -1), (("gx", 1), ("gy", 2)), 1)
    return jnp.sum(spread[:, 0::2, 0::2], axis=(1, 2))


def orthogonalize(image, basis):
    coeffs = []
    for vector in basis:
        coeff = lax.psum(jnp.sum(image * vector), ("gx", "gy"))
        image = image - coeff * vector
        coeffs.append(coeff)
    return (image, coeffs)


def least_squares(top_first, sub_first, top_second, mid_second, sub_second, beta):
    gram_first = top_first * top_first + sub_first * sub_first
    gram_cross = top_first * top_second + sub_first * mid_second
    gram_second = top_second * top_second + mid_second * mid_second + sub_second * sub_second
    determinant = gram_first * gram_second - gram_cross * gram_cross
    weight_one = (gram_second * beta * top_first - gram_cross * beta * top_second) / determinant
    weight_two = (gram_first * beta * top_second - gram_cross * beta * top_first) / determinant
    return (weight_one, weight_two)


def body(
    right_side,
    diag_blocks,
    off_blocks,
    cell_inverse,
    send_cells,
    recv_index,
    seg_count,
    span_inverse,
    span_couple,
):
    cell_shape = right_side.shape
    send_list = send_cells[0]
    recv_list = recv_index.reshape(-1)
    alive = (jnp.arange(MAXSEG)[None, :] < seg_count[:, None]).reshape(1, -1)
    inverse_flat = cell_inverse.reshape(9, -1)
    perforated = jnp.take(diag_blocks.reshape(9, -1), send_list, axis=1)
    owner_blocks = jnp.take(gather_blocks(perforated), recv_list, axis=1)
    beta = jnp.sqrt(lax.psum(jnp.sum(right_side * right_side), ("gx", "gy")))
    basis = [right_side / beta]
    search = []
    entries = []
    for column in range(2):
        flat = basis[column].reshape(3, -1)
        result = block_apply(inverse_flat, flat)
        picked = jnp.take(flat, send_list, axis=1)
        arrived = jnp.take(gather_values(picked), recv_list, axis=1)
        arrived = block_apply(owner_blocks, arrived)
        segments = jnp.where(alive, arrived, 0.0)
        solved = jnp.where(alive, chain_solve(segments, span_inverse, span_couple), 0.0)
        slots = jnp.zeros((3, 9 * picked.shape[1]), jnp.float32).at[:, recv_list].add(solved)
        returned = return_values(slots)
        direction = result.at[:, send_list].add(returned).reshape(cell_shape)
        search.append(direction)
        image = apply_jacobian(direction, diag_blocks, off_blocks)
        image, coeffs = orthogonalize(image, basis)
        size = jnp.sqrt(lax.psum(jnp.sum(image * image), ("gx", "gy")))
        entries.append((coeffs, size))
        basis.append(image / size)
    top_first, sub_first = (entries[0][0][0], entries[0][1])
    top_second, mid_second, sub_second = (entries[1][0][0], entries[1][0][1], entries[1][1])
    weight_one, weight_two = least_squares(
        top_first, sub_first, top_second, mid_second, sub_second, beta
    )
    solution = weight_one * search[0] + weight_two * search[1]
    residual = (
        (beta - top_first * weight_one - top_second * weight_two) * basis[0]
        - (sub_first * weight_one + mid_second * weight_two) * basis[1]
        - sub_second * weight_two * basis[2]
    )
    return (solution, residual)


def solution(mesh):
    return jax.shard_map(
        body,
        mesh=mesh,
        in_specs=(
            P(None, "gx", "gy", None),
            P(None, "gx", "gy", None),
            P(None, None, "gx", "gy", None),
            P(None, "gx", "gy", None),
            P(("gx", "gy"), None),
            P(("gx", "gy"), None),
            P(("gx", "gy")),
            P(None, None, ("gx", "gy")),
            P(None, None, ("gx", "gy")),
        ),
        out_specs=(P(None, "gx", "gy", None), P(None, "gx", "gy", None)),
        check_vma=False,
    )
```

profile of v0, /device:TPU:0, one launch (start us, length us, event | category | flops | bytes accessed | tf_op | source)
XLA Modules:
  0.0 992.2 jit_solution(7060741377387790634)
XLA Ops:
  3.0 68.3 %psum.42 = f32[]{:T(128)} all-reduce(f32[]{:T(128)} %multiply_reduce_fusion.5), channel_id=1, replica_groups=mesh['gx'=32,'gy'=4] {'gx','gy'}, use_global_device_ids=true, to_apply=%region_1.2 | all-reduce | flops 1 | bytes 8 | tf_op jit(solution)/shard_map/psum | solution.py:137
  72.9 4.6 copy.322
  78.2 9.0 gather_fusion.2
  89.3 2.1 collective-permute-start.4
  92.8 4.7 copy.317
  97.5 9.0 gather_fusion
  109.3 3.0 collective-permute-start
  117.3 3.6 reshape.917
  122.7 2.3 collective-permute-start.6
  127.3 5.3 collective-permute-start.2
  135.2 7.5 copy.326
  142.8 10.8 %gather_fusion.3 = f32[3200,3]{1,0:T(8,128)S(1)} fusion(f32[3,28800]{0,1:T(8,128)} %bitcast.704, s32[4096]{0:T(1024)S(1)} %copy-done.22), kind=kCustom, calls=%fused_computation.1.clone | custom fusion | bytes 89600 | tf_op jit(solution)/shard_map/jit(_take)/gather | solution.py:145
  157.3 7.7 copy.321
  165.0 12.2 %gather_fusion.1 = f32[3200,9]{1,0:T(8,128)} fusion(f32[9,28800]{0,1:T(8,128)} %bitcast.702, s32[4096]{0:T(1024)S(1)} %copy-done.29), kind=kCustom, calls=%fused_computation.5 | custom fusion | bytes 243200 | tf_op jit(solution)/shard_map/jit(_take)/gather | solution.py:136
  177.1 2.8 select_bitcast_fusion.4
  179.9 5.7 add_reduce_fusion.5
  188.1 33.0 %while.24 = (s32[]{:T(128)}, f32[3,8]{0,1:T(8,128)S(1)}, f32[25,48,8]{1,2,0:T(8,128)S(1)}, f32[25,48,8,48]{3,2,1,0:T(8,128)}, f32[25,48,8]{2,1,0:T(8,128)S(1)}, ...) while((s32[]{:T(128)}, f32[3,8]{0,1:T(8,128)S(1)}, ...), condition=%wide.region_4.7_spmd, body=%wide.region_2.0_spmd.sunk | while | flops 37066 | bytes 92397 | solution.py:74
  223.7 26.3 %scatter_custom_fusion = f32[3,28800]{0,1:T(8,128)} fusion(s32[3200]{0:T(1024)} %copy-done.31, f32[3200,3]{1,0:T(8,128)S(1)} %copy.332, f32[]{:T(128)} %constant.68.clone.1), kind=kCustom, calls=%fused_computation.100 | custom fusion | flops 9600 | bytes 346112 | tf_op jit(solution)/shard_map/scatter-add | solution.py:149
  249.9 8.2 fusion.148
  258.2 3.3 copy.376
  261.5 3.0 collective-permute-start.8
  264.6 3.4 copy.377
  270.2 9.7 copy.336
  282.2 5.0 collective-permute-start.10
  288.6 5.1 copy.341
  298.1 24.7 %scatter_fusion = f32[3,16384]{0,1:T(8,128)} fusion(f32[3,16384]{0,1:T(8,128)} %copy.341, s32[3200]{0:T(1024)S(1)} %copy-done.18, f32[3200,3]{1,0:T(8,128)} %copy.342), kind=kCustom, calls=%fused_computation.7 | custom fusion | flops 9600 | bytes 128000 | tf_op jit(solution)/shard_map/scatter-add | solution.py:151
  322.8 19.5 %slice_reduce_fusion.5 = (f32[16384]{0:T(1024)S(1)}, f32[16384]{0:T(1024)S(1)}, f32[16384]{0:T(1024)S(1)}) fusion(f32[3,16384]{0,1:T(8,128)} %scatter_fusion), kind=kLoop, calls=%fused_computation.97 | loop fusion | bytes 393216 | tf_op jit(solution)/shard_map/slice | solution.py:31
  342.5 5.3 copy.343
  347.8 5.3 collective-permute-start.12
  354.5 3.4 collective-permute-done.13
  358.0 4.4 collective-permute-start.14
  364.7 3.3 collective-permute-done.15
  370.4 74.5 %psum.43 = f32[]{:T(128)} all-reduce(f32[]{:T(128)} %get-tuple-element.208), channel_id=1, replica_groups=mesh['gx'=32,'gy'=4] {'gx','gy'}, use_global_device_ids=true, to_apply=%region_9.12 | all-reduce | flops 1 | bytes 8 | tf_op jit(solution)/shard_map/psum | solution.py:103
  446.1 62.7 %psum.44 = f32[]{:T(128)} all-reduce(f32[]{:T(128)} %multiply_reduce_fusion.3), channel_id=1, replica_groups=mesh['gx'=32,'gy'=4] {'gx','gy'}, use_global_device_ids=true, to_apply=%region_11.14 | all-reduce | flops 1 | bytes 8 | tf_op jit(solution)/shard_map/psum | solution.py:155
  511.1 4.6 copy.348
  515.7 10.4 %gather_fusion.4 = f32[3200,3]{1,0:T(8,128)} fusion(f32[3,16384]{0,1:T(8,128)} %bitcast.707, s32[4096]{0:T(1024)S(1)} %copy-done.24), kind=kCustom, calls=%fused_computation.2.clone | custom fusion | bytes 89600 | tf_op jit(solution)/shard_map/jit(_take)/gather | solution.py:144
  526.1 3.7 select_bitcast_fusion.1
  534.8 2.6 collective-permute-done.17
  538.2 3.0 collective-permute-start.18
  543.2 5.1 collective-permute-done.19
  550.4 8.5 copy.352
  558.9 12.2 %gather_fusion.5 = f32[3200,3]{1,0:T(8,128)} fusion(f32[3,28800]{0,1:T(8,128)} %bitcast.703, s32[4096]{0:T(1024)S(1)} %copy-done.22), kind=kCustom, calls=%fused_computation.3.clone | custom fusion | bytes 89600 | tf_op jit(solution)/shard_map/jit(_take)/gather | solution.py:145
  571.1 2.8 select_bitcast_fusion
  573.9 5.6 add_reduce_fusion.2
  580.4 56.9 %while.25 = (s32[]{:T(128)}, f32[3,8]{0,1:T(8,128)S(1)}, f32[25,48,8]{1,2,0:T(8,128)S(1)}, f32[25,48,8,48]{3,2,1,0:T(8,128)}, f32[25,48,8]{2,1,0:T(8,128)S(1)}, ...) while((s32[]{:T(128)}, f32[3,8]{0,1:T(8,128)S(1)}, ...), condition=%wide.region_14.17_spmd, body=%wide.region_12.16_spmd.sunk | while | flops 37066 | bytes 92397 | solution.py:74
  638.5 26.2 %scatter_custom_fusion.2 = f32[3,28800]{0,1:T(8,128)} fusion(s32[3200]{0:T(1024)} %copy-done.31, f32[3200,3]{1,0:T(8,128)S(1)} %copy.358, f32[]{:T(128)} %constant.68.clone.1), kind=kCustom, calls=%fused_computation.98 | custom fusion | flops 9600 | bytes 346112 | tf_op jit(solution)/shard_map/scatter-add | solution.py:149
  664.7 8.2 fusion.147
  672.9 3.3 copy.378
  676.2 2.8 collective-permute-start.20
  679.1 3.3 copy.379
  684.0 9.0 copy.362
  693.6 3.1 collective-permute-start.22
  699.4 5.1 copy.367
  707.6 24.7 %scatter_fusion.1 = f32[3,16384]{0,1:T(8,128)} fusion(f32[3,16384]{0,1:T(8,128)} %copy.367, s32[3200]{0:T(1024)S(1)} %copy-done.18, f32[3200,3]{1,0:T(8,128)S(1)} %copy.368), kind=kCustom, calls=%fused_computation.9 | custom fusion | flops 9600 | bytes 128000 | tf_op jit(solution)/shard_map/scatter-add | solution.py:151
  732.3 19.1 %slice_reduce_fusion.2 = (f32[16384]{0:T(1024)S(1)}, f32[16384]{0:T(1024)S(1)}, f32[16384]{0:T(1024)S(1)}) fusion(f32[3,16384]{0,1:T(8,128)} %scatter_fusion.1), kind=kLoop, calls=%fused_computation.94 | loop fusion | bytes 393216 | tf_op jit(solution)/shard_map/slice | solution.py:31
  751.6 5.2 copy.369
  756.8 5.1 collective-permute-start.24
  763.3 3.3 collective-permute-done.25
  766.6 4.5 collective-permute-start.26
  773.5 3.3 collective-permute-done.27
  778.6 71.1 %psum.45 = f32[]{:T(128)} all-reduce(f32[]{:T(128)} %get-tuple-element.190), channel_id=1, replica_groups=mesh['gx'=32,'gy'=4] {'gx','gy'}, use_global_device_ids=true, to_apply=%region_19.22 | all-reduce | flops 1 | bytes 8 | tf_op jit(solution)/shard_map/psum | solution.py:103
  852.4 62.4 %psum.46 = f32[]{:T(128)} all-reduce(f32[]{:T(128)} %multiply_reduce_fusion.1), channel_id=1, replica_groups=mesh['gx'=32,'gy'=4] {'gx','gy'}, use_global_device_ids=true, to_apply=%region_21.24 | all-reduce | flops 1 | bytes 8 | tf_op jit(solution)/shard_map/psum | solution.py:103
  921.0 64.7 %psum.47 = f32[]{:T(128)} all-reduce(f32[]{:T(128)} %multiply_reduce_fusion), channel_id=1, replica_groups=mesh['gx'=32,'gy'=4] {'gx','gy'}, use_global_device_ids=true, to_apply=%region_23.26 | all-reduce | flops 1 | bytes 8 | tf_op jit(solution)/shard_map/psum | solution.py:155
  989.6 2.1 multiply_subtract_fusion
  (630 shorter events, 165.0 us)
Async XLA Ops:
  3.0 103.5 %copy-start.27 = (pred[3200]{0:T(1024)(128)(4,1)}, pred[3200]{0:T(1024)(128)(4,1)S(1)}, u32[]{:S(2)}) copy-start(pred[3200]{0:T(1024)(128)(4,1)S(1)} %compare_and_fusion) | copy-start | bytes 9604
  72.9 4.7 copy-start.8
  77.6 0.6 copy-start.23
  88.8 3.9 copy-start.32
  88.8 4.0 copy-start.3
  89.3 32.5 %collective-permute-start.4 = (f32[3,1,1,3200]{3,2,1,0:T(1,128)S(1)}, f32[3,1,1,3200]{3,2,1,0:T(1,128)}, u32[]{:S(2)}, u32[]{:S(2)}) collective-permute-start(f32[3,1,1,3200]{3,2,1,0:T(1,128)S(1)} %copy.323), channel_id=1, source_target_pairs={{0,4},{4,8},{8,12},{12,16},{16,20},{20,24},{24,28},{28,32},{32,36}... | collective-permute-start | bytes 115208 | tf_op jit(solution)/shard_map/ppermute | solution.py:19
  91.5 30.3 %collective-permute-start.5 = (f32[3,1,1,3200]{3,2,1,0:T(1,128)S(1)}, f32[3,1,1,3200]{3,2,1,0:T(1,128)}, u32[]{:S(2)}, u32[]{:S(2)}) collective-permute-start(f32[3,1,1,3200]{3,2,1,0:T(1,128)S(1)} %copy.323), channel_id=1, source_target_pairs={{4,0},{8,4},{12,8},{16,12},{20,16},{24,20},{28,24},{32,28},{36,32}... | collective-permute-start | bytes 115208 | tf_op jit(solution)/shard_map/ppermute | solution.py:21
  92.8 4.7 copy-start.17
  106.5 7.2 copy-start.30
  108.2 9.1 copy-start.6
  109.3 16.9 %collective-permute-start = (f32[9,1,1,3200]{3,2,1,0:T(1,128)}, f32[9,1,1,3200]{3,2,1,0:T(1,128)S(1)}, u32[]{:S(2)}, u32[]{:S(2)}) collective-permute-start(f32[9,1,1,3200]{3,2,1,0:T(1,128)} %copy.318), channel_id=1, source_target_pairs={{0,4},{4,8},{8,12},{12,16},{16,20},{20,24},{24,28},{28,32},{32,36}... | collective-permute-start | bytes 345608 | tf_op jit(solution)/shard_map/ppermute | solution.py:19
  112.4 13.9 %collective-permute-start.1 = (f32[9,1,1,3200]{3,2,1,0:T(1,128)}, f32[9,1,1,3200]{3,2,1,0:T(1,128)S(1)}, u32[]{:S(2)}, u32[]{:S(2)}) collective-permute-start(f32[9,1,1,3200]{3,2,1,0:T(1,128)} %copy.318), channel_id=1, source_target_pairs={{4,0},{8,4},{12,8},{16,12},{20,16},{24,20},{28,24},{32,28},{36,32}... | collective-permute-start | bytes 345608 | tf_op jit(solution)/shard_map/ppermute | solution.py:21
  116.6 4.3 copy-start.31
  117.3 3.6 copy-start.33
  117.3 9.0 copy-start.10
  122.7 11.4 %collective-permute-start.6 = (f32[3,3,1,3200]{3,2,1,0:T(1,128)S(1)}, f32[3,3,1,3200]{3,2,1,0:T(1,128)S(1)}, u32[]{:S(2)}, u32[]{:S(2)}) collective-permute-start(f32[3,3,1,3200]{3,2,1,0:T(1,128)S(1)} %pad_maximum_fusion.12), channel_id=1, source_target_pairs={{0,1},{1,2},{2,3},{4,5},{5,6},{6,7},{8,9},{9,10},{10,11},{12,13},{... | collective-permute-start | bytes 345608 | tf_op jit(solution)/shard_map/ppermute | solution.py:19
  125.0 9.1 collective-permute-start.7
  126.3 7.8 copy-start.12
  126.3 7.8 copy-start.14
  127.3 27.9 %collective-permute-start.2 = (f32[9,3,1,3200]{3,2,1,0:T(1,128)}, f32[9,3,1,3200]{3,2,1,0:T(1,128)}, u32[]{:S(2)}, u32[]{:S(2)}) collective-permute-start(f32[9,3,1,3200]{3,2,1,0:T(1,128)} %pad_maximum_fusion.9), channel_id=1, source_target_pairs={{0,1},{1,2},{2,3},{4,5},{5,6},{6,7},{8,9},{9,10},{10,11},{12,13},{... | collective-permute-start | bytes 1036808 | tf_op jit(solution)/shard_map/ppermute | solution.py:19
  132.6 22.7 %collective-permute-start.3 = (f32[9,3,1,3200]{3,2,1,0:T(1,128)}, f32[9,3,1,3200]{3,2,1,0:T(1,128)}, u32[]{:S(2)}, u32[]{:S(2)}) collective-permute-start(f32[9,3,1,3200]{3,2,1,0:T(1,128)} %pad_maximum_fusion.9), channel_id=1, source_target_pairs={{1,0},{2,1},{3,2},{5,4},{6,5},{7,6},{9,8},{10,9},{11,10},{13,12},{... | collective-permute-start | bytes 1036808 | tf_op jit(solution)/shard_map/ppermute | solution.py:21
  135.2 7.6 copy-start.22
  135.2 18.3 %copy-start.25 = (pred[3200]{0:T(1024)(128)(4,1)S(1)}, pred[3200]{0:T(1024)(128)(4,1)}, u32[]{:S(2)}) copy-start(pred[3200]{0:T(1024)(128)(4,1)} %compare_and_fusion.1) | copy-start | bytes 9604
  153.6 1.7 copy-start.11
  153.6 1.7 copy-start.13
  153.6 1.7 copy-start.15
  157.3 7.7 copy-start.29
  188.1 33.6 %copy-start.34 = (pred[3200]{0:T(1024)(128)(4,1)S(1)}, pred[3200]{0:T(1024)(128)(4,1)}, u32[]{:S(2)}) copy-start(pred[3200]{0:T(1024)(128)(4,1)} %lt.96) | copy-start | bytes 9604
  221.1 28.8 %copy-start.16 = (f32[25,9,8]{2,1,0:T(8,128)}, f32[25,9,8]{2,1,0:T(8,128)S(1)}, u32[]{:S(2)}) copy-start(f32[25,9,8]{2,1,0:T(8,128)S(1)} %get-tuple-element.501) | copy-start | bytes 21604
  261.5 18.4 %collective-permute-start.8 = (f32[3,1,3,3200]{3,1,2,0:T(1,128)S(1)}, f32[3,1,3,3200]{3,1,2,0:T(1,128)S(1)}, u32[]{:S(2)}, u32[]{:S(2)}) collective-permute-start(f32[3,1,3,3200]{3,1,2,0:T(1,128)S(1)} %copy.376), channel_id=1, source_target_pairs={{0,4},{4,8},{8,12},{12,16},{16,20},{20,24},{24,28},{28,32},{32,36}... | collective-permute-start | bytes 345608 | tf_op jit(solution)/shard_map/ppermute | solution.py:19
  264.5 4.7 copy-start.5
  264.5 4.7 copy-start.9
  267.9 12.0 %collective-permute-start.9 = (f32[3,1,3,3200]{3,1,2,0:T(1,128)S(1)}, f32[3,1,3,3200]{3,1,2,0:T(1,128)S(1)}, u32[]{:S(2)}, u32[]{:S(2)}) collective-permute-start(f32[3,1,3,3200]{3,1,2,0:T(1,128)S(1)} %copy.377), channel_id=1, source_target_pairs={{4,0},{8,4},{12,8},{16,12},{20,16},{24,20},{28,24},{32,28},{36,32}... | collective-permute-start | bytes 345608 | tf_op jit(solution)/shard_map/ppermute | solution.py:21
  279.9 8.6 copy-start.19
  282.2 11.7 %collective-permute-start.10 = (f32[3,5,1,3200]{3,2,1,0:T(1,128)}, f32[3,5,1,3200]{3,2,1,0:T(1,128)}, u32[]{:S(2)}, u32[]{:S(2)}) collective-permute-start(f32[3,5,1,3200]{3,2,1,0:T(1,128)} %get-tuple-element.294), channel_id=1, source_target_pairs={{0,1},{1,2},{2,3},{4,5},{5,6},{6,7},{8,9},{9,10},{10,11},{12,13},{... | collective-permute-start | bytes 576008 | tf_op jit(solution)/shard_map/ppermute | solution.py:19
  287.2 7.8 collective-permute-start.11
  296.3 1.9 copy-start.18
  342.5 12.0 %copy-start.4 = (f32[9,4,16,256]{3,2,1,0:T(8,128)S(1)}, f32[9,4,16,256]{3,2,1,0:T(8,128)}, u32[]{:S(2)}) copy-start(f32[9,4,16,256]{3,2,1,0:T(8,128)} %param.18) | copy-start | bytes 1769476
  347.8 20.6 %copy-start.1 = (f32[6,9,4,16,256]{4,3,2,1,0:T(8,128)S(1)}, f32[6,9,4,16,256]{4,3,2,1,0:T(8,128)}, u32[]{:S(2)}) copy-start(f32[6,9,4,16,256]{4,3,2,1,0:T(8,128)} %param.19) | copy-start | bytes 10616836
  347.8 6.7 collective-permute-start.12
  353.1 4.8 collective-permute-start.13
  358.0 6.7 collective-permute-start.14
  362.4 5.7 collective-permute-start.15
  368.7 0.9 copy-start
  370.4 138.4 %copy-start.7 = (f32[3,4,16,256]{3,2,1,0:T(8,128)}, f32[3,4,16,256]{3,2,1,0:T(8,128)S(1)}, u32[]{:S(2)}) copy-start(f32[3,4,16,256]{3,2,1,0:T(8,128)S(1)} %get-tuple-element.209) | copy-start | bytes 589828
  511.1 4.7 copy-start.24
  511.1 15.0 %copy-start.28 = (pred[3200]{0:T(1024)(128)(4,1)S(1)}, pred[3200]{0:T(1024)(128)(4,1)}, u32[]{:S(2)}) copy-start(pred[3200]{0:T(1024)(128)(4,1)} %copy-done.27) | copy-start | bytes 9604
  531.7 3.1 collective-permute-start.16
  533.5 4.0 collective-permute-start.17
  534.8 2.6 copy-start.20
  537.4 0.8 copy-start.21
  538.2 5.0 collective-permute-start.18
  541.2 7.1 collective-permute-start.19
  550.4 20.7 %copy-start.26 = (pred[3200]{0:T(1024)(128)(4,1)S(1)}, pred[3200]{0:T(1024)(128)(4,1)}, u32[]{:S(2)}) copy-start(pred[3200]{0:T(1024)(128)(4,1)} %compare_and_fusion.1) | copy-start | bytes 9604
  580.4 57.5 %copy-start.35 = (pred[3200]{0:T(1024)(128)(4,1)S(1)}, pred[3200]{0:T(1024)(128)(4,1)}, u32[]{:S(2)}) copy-start(pred[3200]{0:T(1024)(128)(4,1)} %lt.96) | copy-start | bytes 9604
  676.2 16.7 %collective-permute-start.20 = (f32[3,1,3,3200]{3,1,2,0:T(1,128)S(1)}, f32[3,1,3,3200]{3,1,2,0:T(1,128)S(1)}, u32[]{:S(2)}, u32[]{:S(2)}) collective-permute-start(f32[3,1,3,3200]{3,1,2,0:T(1,128)S(1)} %copy.378), channel_id=1, source_target_pairs={{0,4},{4,8},{8,12},{12,16},{16,20},{20,24},{24,28},{28,32},{32,36}... | collective-permute-start | bytes 345608 | tf_op jit(solution)/shard_map/ppermute | solution.py:19
  682.4 10.7 %collective-permute-start.21 = (f32[3,1,3,3200]{3,1,2,0:T(1,128)S(1)}, f32[3,1,3,3200]{3,1,2,0:T(1,128)S(1)}, u32[]{:S(2)}, u32[]{:S(2)}) collective-permute-start(f32[3,1,3,3200]{3,1,2,0:T(1,128)S(1)} %copy.379), channel_id=1, source_target_pairs={{4,0},{8,4},{12,8},{16,12},{20,16},{24,20},{28,24},{32,28},{36,32}... | collective-permute-start | bytes 345608 | tf_op jit(solution)/shard_map/ppermute | solution.py:21
  693.6 11.1 %collective-permute-start.22 = (f32[3,5,1,3200]{3,2,1,0:T(1,128)S(1)}, f32[3,5,1,3200]{3,2,1,0:T(1,128)}, u32[]{:S(2)}, u32[]{:S(2)}) collective-permute-start(f32[3,5,1,3200]{3,2,1,0:T(1,128)S(1)} %get-tuple-element.292), channel_id=1, source_target_pairs={{0,1},{1,2},{2,3},{4,5},{5,6},{6,7},{8,9},{9,10},{10,11},{12,13},{... | collective-permute-start | bytes 576008 | tf_op jit(solution)/shard_map/ppermute | solution.py:19
  696.7 9.0 collective-permute-start.23
  756.8 20.4 %copy-start.2 = (f32[6,9,4,16,256]{4,3,2,1,0:T(8,128)S(1)}, f32[6,9,4,16,256]{4,3,2,1,0:T(8,128)}, u32[]{:S(2)}) copy-start(f32[6,9,4,16,256]{4,3,2,1,0:T(8,128)} %param.19) | copy-start | bytes 10616836
  756.8 6.5 collective-permute-start.24
  761.9 4.6 collective-permute-start.25
  766.6 6.9 collective-permute-start.26
  771.1 5.7 collective-permute-start.27
where the time goes:
time: 1000 us; the launch traced here: 992 us
  blocking collectives  404 us (40%)
  local copies, waits for them, and re-layouts  243 us (24%)
  other arithmetic  238 us (24%)
  starting transfers between devices  68.9 us (7%)
  waiting for transfers between devices  21.8 us (2%)
  between operations  14.8 us (1%)
    psum x3, blocking collectives, orthogonalize(): coeff = lax.psum(jnp.sum(image * vector), ('gx', 'gy'))  208 us
    psum x2, blocking collectives, body(): size = jnp.sqrt(lax.psum(jnp.sum(image * image), ('gx', 'gy')))  127 us
    psum x1, blocking collectives, body(): beta = jnp.sqrt(lax.psum(jnp.sum(right_side * right_side), ('gx', 'gy')))  68.3 us
    reduce_sum x50, other arithmetic, advance(): solved = jnp.sum(block_inverse * block_rhs[:, :, None], axis=0).T  52.6 us
    scatter-add x2, other arithmetic, body(): jnp.zeros((3, 9 * picked.shape[1]), jnp.float32).at[:, recv_list]  52.5 us
    ppermute x14, starting transfers between devices, with_halo(): lax.ppermute(tail, axis, [(i, (i + 1) % count) for i in range(ends)])  50.7 us
    scatter-add x2, other arithmetic, body(): direction = result.at[:, send_list].add(returned).reshape(cell_shape)  49.4 us
    add x70, other arithmetic, block_apply(): matrix[3 * a] * vector[0] + matrix[3 * a + 1] * vector[1]  40.1 us
  transfers between devices with their start and end apart: 28, of which 8 were waited for; matrix products, arithmetic and copies ran while one was open for 9% of the time, Pallas kernels for 0%

commit v1 on v0

v1 whole, which is shorter than its diff:
```python
import functools

import jax
import jax.numpy as jnp
import numpy as np
from jax import lax
from jax.experimental import pallas as pl
from jax.experimental.pallas import tpu as pltpu
from jax.sharding import PartitionSpec as P

CX, CY, CZ = 4, 16, 256
WELLS = 8
MAXSEG = 400
SPAN = 16
NCHUNK = 25
WIDTH = 3 * SPAN
LANES = WELLS * WIDTH
ROWS = 25
MESH = pl.DeviceIdType.MESH
F32, BF16, I32 = jnp.float32, jnp.bfloat16, jnp.int32
NEAR = [(a, b) for a in (-1, 0, 1) for b in (-1, 0, 1)]
ORDER = [7, 1, 3, 5, 6, 8, 0, 2]


def expand_matrix():
    row = np.arange(9 * WELLS)
    lane = np.arange(3 * LANES)
    same = (row[:, None] // WELLS % 3 == lane[None] // LANES) & (
        row[:, None] % WELLS == lane[None] % LANES // WIDTH
    )
    return same.astype(np.float32)


def permute_matrix():
    lane = np.arange(LANES)
    well, segment, part = lane // WIDTH, lane % WIDTH // 3, lane % 3
    goal = part * 128 + well * SPAN + segment
    return (goal[:, None] == lane[None]).astype(np.float32)


def split3(x):
    first = x.astype(BF16).astype(F32)
    rest = x - first
    second = rest.astype(BF16).astype(F32)
    return first, second, rest - second


def lane_pick(row, lane):
    spread = jnp.broadcast_to(row, lane.shape)
    return jnp.take_along_axis(spread, lane, axis=1, mode="promise_in_bounds")


def kernel(
    n_gx,
    n_gy,
    rhs,
    diag,
    off_hbm,
    cinv_hbm,
    send,
    recv,
    seg_count,
    ginv_hbm,
    couple,
    expand,
    permute,
    sol,
    res,
    off,
    cinv,
    ginv,
    field,
    u,
    zp,
    ystage,
    yhalo,
    pool,
    slots,
    back,
    ret,
    cell,
    seg_row,
    seg_lane,
    inv_row,
    inv_lane,
    cell_row,
    cell_lane,
    spread,
    y0,
    yp,
    chain,
    ends,
    ytab,
    cpad,
    ar1,
    ar2,
    load_sem,
    fwd_send,
    fwd_recv,
    back_send,
    back_recv,
    halo_send,
    halo_recv,
    ar1_send,
    ar1_recv,
    ar2_send,
    ar2_recv,
):
    ix = lax.axis_index("gx")
    iy = lax.axis_index("gy")
    core = lax.rem(ix, 2)
    chip = lax.div(ix, 2)
    chips = n_gx // 2
    near = 2 * n_gy

    loads = [
        pltpu.make_async_copy(cinv_hbm, cinv, load_sem.at[0]),
        pltpu.make_async_copy(off_hbm, off, load_sem.at[1]),
    ] + [
        pltpu.make_async_copy(
            ginv_hbm.at[:, j * 128 : j * 128 + 128], ginv.at[j], load_sem.at[2 + j]
        )
        for j in range(3)
    ]
    for load in loads:
        load.start()

    def exists(q):
        a, b = NEAR[q]
        good = True
        if a < 0:
            good = ix > 0
        elif a > 0:
            good = ix < n_gx - 1
        if b < 0:
            good = good & (iy > 0)
        elif b > 0:
            good = good & (iy < n_gy - 1)
        return good

    def device(q):
        return (ix + NEAR[q][0], iy + NEAR[q][1])

    def near_device(d):
        place = lax.rem(core * n_gy + iy + d, near)
        return (chip * 2 + lax.div(place, n_gy), lax.rem(place, n_gy))

    def far_device(d):
        return (lax.rem(chip + d, chips) * 2 + core, iy)

    barrier = pltpu.get_barrier_semaphore()
    for q in ORDER:

        @pl.when(exists(q))
        def _(q=q):
            pl.semaphore_signal(barrier, inc=1, device_id=device(q), device_id_type=MESH)

    for d in range(1, near):
        pl.semaphore_signal(barrier, inc=1, device_id=near_device(d), device_id_type=MESH)
    for d in range(1, chips):
        pl.semaphore_signal(barrier, inc=1, device_id=far_device(d), device_id_type=MESH)

    def present(edge):
        return jnp.where(edge, 1, 0)

    across_x = 1 + present(ix > 0) + present(ix < n_gx - 1)
    across_y = 1 + present(iy > 0) + present(iy < n_gy - 1)
    greeted = across_x * across_y - 1 + (near - 1) + (chips - 1)

    def fwd_copy(it, q):
        return pltpu.make_async_remote_copy(
            src_ref=pool.at[it, 4],
            dst_ref=pool.at[it, 8 - q],
            send_sem=fwd_send.at[it, q],
            recv_sem=fwd_recv.at[it, 8 - q],
            device_id=device(q),
            device_id_type=MESH,
        )

    def back_copy(it, q):
        return pltpu.make_async_remote_copy(
            src_ref=slots.at[it, q],
            dst_ref=back.at[it, 8 - q],
            send_sem=back_send.at[it, q],
            recv_sem=back_recv.at[it, 8 - q],
            device_id=device(q),
            device_id_type=MESH,
        )

    side_place = [1, 7, 3, 5]

    def halo_copy(it, side):
        if side < 2:
            src = zp.at[it, 1 if side == 0 else CX]
            dst = zp.at[it, CX + 1 if side == 0 else 0]
        else:
            src = ystage.at[it, side - 2]
            dst = yhalo.at[it, 3 - side]
        other = side ^ 1
        return pltpu.make_async_remote_copy(
            src_ref=src,
            dst_ref=dst,
            send_sem=halo_send.at[it, side],
            recv_sem=halo_recv.at[it, other],
            device_id=device(side_place[side]),
            device_id_type=MESH,
        )

    def near_copy(i, d):
        return pltpu.make_async_remote_copy(
            src_ref=ar1.at[i, 0],
            dst_ref=ar1.at[i, d],
            send_sem=ar1_send.at[i, d],
            recv_sem=ar1_recv.at[i, d],
            device_id=near_device(d),
            device_id_type=MESH,
        )

    def far_copy(i, d):
        return pltpu.make_async_remote_copy(
            src_ref=ar2.at[i, 0],
            dst_ref=ar2.at[i, d],
            send_sem=ar2_send.at[i, d],
            recv_sem=ar2_recv.at[i, d],
            device_id=far_device(d),
            device_id_type=MESH,
        )

    def send_near(i):
        for d in range(1, near):
            near_copy(i, d).start()

    def pass_on(i):
        total = ar1[i, 0]
        for d in range(1, near):
            near_copy(i, d).wait_recv()
            total = total + ar1[i, d]
        ar2[i, 0] = total
        for d in range(1, chips):
            far_copy(i, d).start()

    def collect(i):
        total = ar2[i, 0]
        for d in range(1, chips):
            far_copy(i, d).wait_recv()
            total = total + ar2[i, d]
        return jnp.sum(total, axis=1, keepdims=True)

    for c in range(ROWS):
        cell[c : c + 1, :] = send[:, c * 128 : (c + 1) * 128]

    field[0] = rhs[...]

    def forward(it):
        for a in range(3):
            total = diag[3 * a] * field[it, 0]
            total = total + diag[3 * a + 1] * field[it, 1]
            total = total + diag[3 * a + 2] * field[it, 2]
            total = total.reshape(CX * CY, CZ)
            u[a, 0] = total[:, :128]
            u[a, 1] = total[:, 128:]
        where = cell[...]
        high = where >> 7
        lane = where & 127

        def step(r, got):
            got = list(got)
            for half in range(2):
                match = high == 2 * r + half
                for a in range(3):
                    row = u[a, half, pl.ds(r, 1), :]
                    got[a] = jnp.where(match, lane_pick(row, lane), got[a])
            return tuple(got)

        none = jnp.zeros((ROWS, 128), F32)
        got = lax.fori_loop(0, CX * CY, step, (none, none, none), unroll=2)
        for a in range(3):
            pool[it, 4, a] = got[a]

    def send_forward(it):
        for q in ORDER:

            @pl.when(exists(q))
            def _(q=q):
                fwd_copy(it, q).start()

    def setup():
        sub64 = lax.broadcasted_iota(I32, (CX * CY, 640), 0)
        sub256 = lax.broadcasted_iota(I32, (CZ, 640), 0)
        lanes = lax.broadcasted_iota(I32, (1, 640), 1)
        total = jnp.zeros((2 * CX * CY, CZ), F32)
        for m in range(5):
            where = send[:, m * 640 : m * 640 + 640]
            slot = lanes + m * 640
            hit = sub64 == (where >> 8)
            row = jnp.where(hit, ((slot >> 7) + 1).astype(F32), 0.0)
            lane = jnp.where(hit, (slot & 127).astype(F32), 0.0)
            left = jnp.concatenate([row, lane], axis=0).astype(BF16)
            right = jnp.where(sub256 == (where & 255), 1.0, 0.0).astype(BF16)
            total = total + lax.dot_general(
                left, right, (((1,), (1,)), ((), ())), preferred_element_type=F32
            )
        cell_row[...] = total[: CX * CY].astype(I32) - 1
        cell_lane[...] = total[CX * CY :].astype(I32)

        seg_lane[...] = jnp.zeros(seg_lane.shape, I32)
        seg_lane[:, :MAXSEG] = recv[...]
        position = seg_lane[...]
        well = lax.broadcasted_iota(I32, (WELLS, 512), 0)
        segment = lax.broadcasted_iota(I32, (WELLS, 512), 1)
        count = jnp.zeros((WELLS, 512), I32)
        for w in range(WELLS):
            count = jnp.where(well == w, seg_count[w], count)
        live = (segment < count) & (segment < MAXSEG)
        high = position >> 7
        seg_row[...] = jnp.where(live, high, -1)
        seg_lane[...] = position & 127

        sub288 = lax.broadcasted_iota(I32, (9 * 32, 512), 0)
        sub128 = lax.broadcasted_iota(I32, (128, 512), 0)
        along = lax.broadcasted_iota(I32, (1, 512), 1)
        total = jnp.zeros((2 * 9 * 32, 128), F32)
        for w in range(WELLS):
            high = seg_row[w : w + 1, :]
            slab = (high * 1311) >> 15
            goal = jnp.where(high < 0, -1, high + 7 * slab)
            hit = sub288 == goal
            row = jnp.where(hit, ((along >> 4) + 1).astype(F32), 0.0)
            lane = jnp.where(hit, ((along & 15) + w * SPAN).astype(F32), 0.0)
            left = jnp.concatenate([row, lane], axis=0).astype(BF16)
            right = jnp.where(sub128 == seg_lane[w : w + 1, :], 1.0, 0.0).astype(BF16)
            total = total + lax.dot_general(
                left, right, (((1,), (1,)), ((), ())), preferred_element_type=F32
            )
        inv_row[...] = total[: 9 * 32].astype(I32) - 1
        inv_lane[...] = total[9 * 32 :].astype(I32)

        cpad[...] = jnp.zeros(cpad.shape, F32)
        for c in range(NCHUNK):
            cpad[16 * c : 16 * c + 9, 0:WELLS] = couple[c]
        for j in range(3):
            loads[2 + j].wait()
        y0[...] = jnp.zeros(y0.shape, F32)
        group = lax.broadcasted_iota(I32, (NCHUNK, 128), 1) >> 4
        firsts = []
        for k in range(3):
            for j in range(3):
                y0[j, 0:NCHUNK] = ginv[j, pl.ds(k, NCHUNK, stride=WIDTH), :]
            firsts.append(permuted())
        pairs = [
            jnp.take_along_axis(
                cpad[pl.ds(kb, NCHUNK, stride=16), :], group, axis=1, mode="promise_in_bounds"
            )
            for kb in range(9)
        ]
        for a in range(3):
            for b in range(3):
                total = firsts[0][:NCHUNK, a * 128 : a * 128 + 128] * pairs[b]
                for k in (1, 2):
                    total = total + firsts[k][:NCHUNK, a * 128 : a * 128 + 128] * pairs[3 * k + b]
                chain[3 * a + b] = total
        for b in range(3):
            ends[b, 0:8] = jnp.zeros((8, 128), F32)

    def permuted():
        rows = jnp.concatenate([y0[j] for j in range(3)], axis=1)
        parts = jnp.concatenate(split3(rows), axis=0).astype(BF16)
        moved = jnp.dot(parts, permute[...], preferred_element_type=F32)
        return moved[0:32] + moved[32:64] + moved[64:96]

    def wells(it):
        row_of = seg_row[...]
        lane_of = seg_lane[...]
        rows4 = [row_of[:, j * 128 : j * 128 + 128] for j in range(4)]
        lanes4 = [lane_of[:, j * 128 : j * 128 + 128] for j in range(4)]
        none = jnp.zeros((WELLS, 128), F32)
        got = tuple([none] * 12)
        for q in [4] + ORDER:
            if q != 4:

                @pl.when(exists(q))
                def _(q=q):
                    fwd_copy(it, 8 - q).wait_recv()

            def step(r, got, q=q):
                got = list(got)
                match = [rows4[j] == q * ROWS + r for j in range(4)]
                for a in range(3):
                    row = pool[it, q, a, pl.ds(r, 1), :]
                    for j in range(4):
                        got[4 * a + j] = jnp.where(
                            match[j], lane_pick(row, lanes4[j]), got[4 * a + j]
                        )
                return tuple(got)

            got = lax.fori_loop(0, ROWS, step, got, unroll=5)
        parts = [split3(jnp.concatenate(got[4 * a : 4 * a + 4], axis=1)) for a in range(3)]
        stack = jnp.concatenate([parts[a][s] for s in range(3) for a in range(3)], axis=0)
        turned = stack.T.astype(BF16)[:MAXSEG]
        spread[...] = jnp.dot(turned, expand[...], preferred_element_type=F32)

        def block(c, carry):
            for j in range(3):
                total = None
                for a in range(3):
                    g = ginv[j, pl.ds(c * WIDTH + a, SPAN, stride=3), :]
                    at = pl.ds(pl.multiple_of(c * SPAN, SPAN), SPAN)
                    r = spread[at, a * LANES + j * 128 : a * LANES + j * 128 + 128]
                    total = g * r if total is None else total + g * r
                y0[j, pl.ds(c, 1), :] = jnp.sum(total, axis=0, keepdims=True)
            return carry

        lax.fori_loop(0, NCHUNK, block, 0, unroll=5)
        moved = permuted()
        for a in range(3):
            yp[a] = moved[:, a * 128 : a * 128 + 128]

        def link(c, last):
            new = []
            for a in range(3):
                value = yp[a, pl.ds(c, 1), :]
                for b in range(3):
                    value = value - chain[3 * a + b, pl.ds(c, 1), :] * last[b]
                new.append(value)
            for a in range(3):
                ends[a, pl.ds(c + 1, 1), :] = new[a]
            return tuple(new)

        lax.fori_loop(0, NCHUNK, link, tuple([jnp.zeros((1, 128), F32)] * 3), unroll=5)
        last_lane = lax.broadcasted_iota(I32, (NCHUNK, 128), 1) | 15
        before = [
            jnp.take_along_axis(
                ends[b, 0:NCHUNK, :], last_lane, axis=1, mode="promise_in_bounds"
            )
            for b in range(3)
        ]
        for a in range(3):
            value = yp[a, 0:NCHUNK]
            for b in range(3):
                value = value - chain[3 * a + b] * before[b]
            ytab[a] = value

        for q in ORDER + [4]:
            row_at = inv_row[q * 32 : q * 32 + ROWS, :]
            lane_at = inv_lane[q * 32 : q * 32 + ROWS, :]

            def step(r, got, row_at=row_at, lane_at=lane_at):
                match = row_at == r
                return tuple(
                    jnp.where(match, lane_pick(ytab[a, pl.ds(r, 1), :], lane_at), got[a])
                    for a in range(3)
                )

            none = jnp.zeros((ROWS, 128), F32)
            got = lax.fori_loop(0, ROWS, step, (none, none, none), unroll=5)
            for a in range(3):
                slots[it, q, a] = got[a]
            if q != 4:

                @pl.when(exists(q))
                def _(q=q):
                    back_copy(it, q).start()

    def backward(it):
        ret[...] = slots[it, 4]
        for q in ORDER:

            @pl.when(exists(q))
            def _(q=q):
                back_copy(it, 8 - q).wait_recv()
                ret[...] = ret[...] + back[it, q]

        def plane(x):
            row_at = cell_row[x * CY : x * CY + CY, :]
            lane_at = cell_lane[x * CY : x * CY + CY, :]
            row_at = [row_at[:, :128], row_at[:, 128:]]
            lane_at = [lane_at[:, :128], lane_at[:, 128:]]

            def step(r, got):
                got = list(got)
                match = [row_at[h] == r for h in range(2)]
                for a in range(3):
                    row = ret[a, pl.ds(r, 1), :]
                    for h in range(2):
                        got[2 * a + h] = jnp.where(
                            match[h], lane_pick(row, lane_at[h]), got[2 * a + h]
                        )
                return tuple(got)

            none = jnp.zeros((CY, 128), F32)
            got = lax.fori_loop(0, ROWS, step, tuple([none] * 6), unroll=5)
            for a in range(3):
                value = jnp.concatenate([got[2 * a], got[2 * a + 1]], axis=1)
                for b in range(3):
                    value = value + cinv[3 * a + b, x] * field[it, b, x]
                zp[it, x + 1, a] = value
                ystage[it, 0, pl.ds(3 * x + a, 1), :] = value[0:1]
                ystage[it, 1, pl.ds(3 * x + a, 1), :] = value[CY - 1 : CY]

        for x in (0, 3, 1, 2):
            plane(x)
            if x == 0:
                start_halo(it, 0)
            if x == 3:
                start_halo(it, 1)
        start_halo(it, 2)
        start_halo(it, 3)

    def start_halo(it, side):
        @pl.when(exists(side_place[side]))
        def _():
            halo_copy(it, side).start()

    def jacobian(it):
        row = lax.broadcasted_iota(I32, (CY, CZ), 0)
        column = lax.broadcasted_iota(I32, (CY, CZ), 1)
        for x in range(CX):
            total = [None] * 3

            def add(blocks, value, b):
                for a in range(3):
                    term = blocks(3 * a + b) * value
                    total[a] = term if total[a] is None else total[a] + term

            for b in range(3):
                here = zp[it, x + 1, b]
                add(lambda e: diag[e, x], here, b)
                if x > 0:
                    add(lambda e: off[0, e, x], zp[it, x, b], b)
                if x < CX - 1:
                    add(lambda e: off[1, e, x], zp[it, x + 2, b], b)
                value = jnp.where(row > 0, pltpu.roll(here, 1, 0), 0.0)
                add(lambda e: off[2, e, x], value, b)
                value = jnp.where(row < CY - 1, pltpu.roll(here, CY - 1, 0), 0.0)
                add(lambda e: off[3, e, x], value, b)
                value = jnp.where(column > 0, pltpu.roll(here, 1, 1), 0.0)
                add(lambda e: off[4, e, x], value, b)
                value = jnp.where(column < CZ - 1, pltpu.roll(here, CZ - 1, 1), 0.0)
                add(lambda e: off[5, e, x], value, b)
            for a in range(3):
                field[it + 1, a, x] = total[a]

        for side in range(4):

            @pl.when(exists(side_place[side]))
            def _(side=side):
                halo_copy(it, side ^ 1).wait_recv()
                if side < 2:
                    x = 0 if side == 0 else CX - 1
                    plane = 0 if side == 0 else CX + 1
                    for a in range(3):
                        value = field[it + 1, a, x]
                        for b in range(3):
                            value = value + off[side, 3 * a + b, x] * zp[it, plane, b]
                        field[it + 1, a, x] = value
                else:
                    y = 0 if side == 2 else CY - 1
                    for x in range(CX):
                        for a in range(3):
                            value = field[it + 1, a, x, y : y + 1, :]
                            for b in range(3):
                                beside = yhalo[it, side - 2, 3 * x + b : 3 * x + b + 1, :]
                                value = value + off[side, 3 * a + b, x, y : y + 1, :] * beside
                            field[it + 1, a, x, y : y + 1, :] = value

    def dot_row(i, place, first, second):
        total = None
        for a in range(3):
            for x in range(CX):
                product = first(a, x) * second(a, x)
                total = product if total is None else total + product
        total = jnp.sum(total, axis=0, keepdims=True)
        ar1[i, 0, place : place + 1, :] = total[:, :128] + total[:, 128:]

    for i in range(2):
        ar1[i, 0] = jnp.zeros((8, 128), F32)

    r_of = lambda a, x: rhs[a, x]
    w1_of = lambda a, x: field[1, a, x]
    w2_of = lambda a, x: field[2, a, x]
    v2_of = lambda a, x: field[0, a, x]

    forward(0)
    pl.semaphore_wait(barrier, greeted)
    send_forward(0)
    setup()
    wells(0)
    loads[0].wait()
    backward(0)
    loads[1].wait()
    jacobian(0)
    forward(1)
    send_forward(1)
    dot_row(0, 0, r_of, r_of)
    dot_row(0, 1, w1_of, r_of)
    send_near(0)
    wells(1)
    pass_on(0)
    backward(1)
    jacobian(1)

    first = collect(0)
    square = first[0:1]
    along = first[1:2] / square
    for a in range(3):
        for x in range(CX):
            field[0, a, x] = field[1, a, x] - along * rhs[a, x]
            field[2, a, x] = field[2, a, x] - along * field[1, a, x]
    dot_row(1, 0, v2_of, v2_of)
    dot_row(1, 1, w2_of, r_of)
    dot_row(1, 2, w2_of, v2_of)
    dot_row(1, 3, w2_of, w2_of)
    dot_row(1, 4, v2_of, r_of)
    send_near(1)
    pass_on(1)
    second = collect(1)

    beta = jnp.sqrt(square)
    size = jnp.sqrt(second[0:1])
    top_first = along
    sub_first = size / beta
    top_second = second[1:2] / (size * beta)
    mid_second = second[2:3] / (size * size) - top_second * (second[4:5] / (size * beta))
    gram_first = top_first * top_first + sub_first * sub_first
    gram_cross = top_first * top_second + sub_first * mid_second
    gram_second = second[3:4] / (size * size)
    determinant = gram_first * gram_second - gram_cross * gram_cross
    weight_one = (gram_second * beta * top_first - gram_cross * beta * top_second) / determinant
    weight_two = (gram_first * beta * top_second - gram_cross * beta * top_first) / determinant
    one = weight_one / beta
    two = weight_two / size
    mixed = one - two * along
    for a in range(3):
        for x in range(CX):
            sol[a, x] = mixed * zp[0, x + 1, a] + two * zp[1, x + 1, a]
            res[a, x] = rhs[a, x] - one * field[1, a, x] - two * field[2, a, x]

    for it in range(2):
        for q in ORDER:

            @pl.when(exists(q))
            def _(it=it, q=q):
                fwd_copy(it, q).wait_send()
                back_copy(it, q).wait_send()

        for side in range(4):

            @pl.when(exists(side_place[side]))
            def _(it=it, side=side):
                halo_copy(it, side).wait_send()

        for d in range(1, near):
            near_copy(it, d).wait_send()
        for d in range(1, chips):
            far_copy(it, d).wait_send()


def body(
    right_side,
    diag_blocks,
    off_blocks,
    cell_inverse,
    send_cells,
    recv_index,
    seg_count,
    span_inverse,
    span_couple,
):
    n_gx, n_gy = lax.axis_size("gx"), lax.axis_size("gy")
    vmem = pl.BlockSpec(memory_space=pltpu.VMEM)
    anywhere = pl.BlockSpec(memory_space=pl.ANY)
    smem = pl.BlockSpec(memory_space=pltpu.SMEM)
    shape = jax.ShapeDtypeStruct(right_side.shape, F32)
    dma = pltpu.SemaphoreType.DMA
    scratch = [
        pltpu.VMEM((6, 9, CX, CY, CZ), F32),
        pltpu.VMEM((9, CX, CY, CZ), F32),
        pltpu.VMEM((3, NCHUNK * WIDTH, 128), F32),
        pltpu.VMEM((3, 3, CX, CY, CZ), F32),
        pltpu.VMEM((3, 2, CX * CY, 128), F32),
        pltpu.VMEM((2, CX + 2, 3, CY, CZ), F32),
        pltpu.VMEM((2, 2, 12, CZ), F32),
        pltpu.VMEM((2, 2, 12, CZ), F32),
        pltpu.VMEM((2, 9, 3, ROWS, 128), F32),
        pltpu.VMEM((2, 9, 3, ROWS, 128), F32),
        pltpu.VMEM((2, 9, 3, ROWS, 128), F32),
        pltpu.VMEM((3, ROWS, 128), F32),
        pltpu.VMEM((ROWS, 128), I32),
        pltpu.VMEM((WELLS, 512), I32),
        pltpu.VMEM((WELLS, 512), I32),
        pltpu.VMEM((9 * 32, 128), I32),
        pltpu.VMEM((9 * 32, 128), I32),
        pltpu.VMEM((CX * CY, CZ), I32),
        pltpu.VMEM((CX * CY, CZ), I32),
        pltpu.VMEM((MAXSEG, 3 * LANES), F32),
        pltpu.VMEM((3, 32, 128), F32),
        pltpu.VMEM((3, 32, 128), F32),
        pltpu.VMEM((9, NCHUNK, 128), F32),
        pltpu.VMEM((3, 32, 128), F32),
        pltpu.VMEM((3, NCHUNK, 128), F32),
        pltpu.VMEM((16 * NCHUNK, 128), F32),
        pltpu.VMEM((2, 2 * n_gy, 8, 128), F32),
        pltpu.VMEM((2, n_gx // 2, 8, 128), F32),
        dma((5,)),
        dma((2, 9)),
        dma((2, 9)),
        dma((2, 9)),
        dma((2, 9)),
        dma((2, 4)),
        dma((2, 4)),
        dma((2, 2 * n_gy)),
        dma((2, 2 * n_gy)),
        dma((2, n_gx // 2)),
        dma((2, n_gx // 2)),
    ]
    return pl.pallas_call(
        functools.partial(kernel, n_gx, n_gy),
        out_shape=(shape, shape),
        in_specs=[vmem, vmem, anywhere, anywhere, vmem, vmem, smem, anywhere, vmem, vmem, vmem],
        out_specs=(vmem, vmem),
        scratch_shapes=scratch,
        compiler_params=pltpu.CompilerParams(collective_id=0, has_side_effects=True),
        name="gmres",
    )(
        right_side,
        diag_blocks,
        off_blocks,
        cell_inverse,
        send_cells,
        recv_index,
        seg_count,
        span_inverse.reshape(NCHUNK * WIDTH, LANES),
        span_couple,
        jnp.asarray(expand_matrix(), BF16),
        jnp.asarray(permute_matrix(), BF16),
    )


def solution(mesh):
    return jax.shard_map(
        body,
        mesh=mesh,
        in_specs=(
            P(None, "gx", "gy", None),
            P(None, "gx", "gy", None),
            P(None, None, "gx", "gy", None),
            P(None, "gx", "gy", None),
            P(("gx", "gy"), None),
            P(("gx", "gy"), None),
            P(("gx", "gy")),
            P(None, None, ("gx", "gy")),
            P(None, None, ("gx", "gy")),
        ),
        out_specs=(P(None, "gx", "gy", None), P(None, "gx", "gy", None)),
        check_vma=False,
    )
```

time: 1000 us -> 104 us (0.10)
  blocking collectives: 404 us -> 0 us
  local copies, waits for them, and re-layouts: 243 us -> 4.85 us
  other arithmetic: 238 us -> 0 us
  Pallas kernels: 0 us -> 97.9 us
  starting transfers between devices: 68.9 us -> 0 us
  waiting for transfers between devices: 21.8 us -> 0 us
  between operations: 14.8 us -> 0.64 us
    psum x6 -> x0, blocking collectives: 404 us -> none  [the longest x3 208 us: orthogonalize(): coeff = lax.psum(jnp.sum(image * vector), ('gx', 'gy'))]
    scatter-add x4 -> x0, other arithmetic: 102 us -> none  [the longest x2 52.5 us: body(): jnp.zeros((3, 9 * picked.shape[1]), jnp.float32).at[:, recv_list]]
    pallas_call x0 -> x1, Pallas kernels: none -> 97.9 us  [body(): pl.pallas_call(functools.partial(kernel, n_gx, n_gy), out_shape=(shape, s...]
    ppermute x28 -> x0, starting transfers between devices: 68.9 us -> none  [the longest x14 50.7 us: with_halo(): lax.ppermute(tail, axis, [(i, (i + 1) % count) for i in range(ends)])]
    gather x6 -> x0, local copies, waits for them, and re-layouts: 63.3 us -> none  [the longest x2 22.9 us: body(): arrived = jnp.take(gather_values(picked), recv_list, axis=1)]
    slice x108 -> x0, local copies, waits for them, and re-layouts: 60.8 us -> none  [the longest x2 38.7 us: block_apply(): vector[0]]
    reduce_sum x58 -> x0, other arithmetic: 60.4 us -> none  [the longest x50 52.6 us: advance(): solved = jnp.sum(block_inverse * block_rhs[:, :, None], axis=0).T]
    add x70 -> x0, other arithmetic: 40.1 us -> none  [block_apply(): matrix[3 * a] * vector[0] + matrix[3 * a + 1] * vector[1]]
  transfers between devices with their start and end apart: 28 -> 0, of which waited for: 8 -> 0; matrix products, arithmetic and copies ran while one was open for 9% -> 0% of each run, Pallas kernels for 0% -> 0%
where the time goes in v1:
time: 104 us; the launch traced here: 103 us
  Pallas kernels  97.9 us (94%)
  local copies, waits for them, and re-layouts  4.85 us (5%)
    pallas_call x1, Pallas kernels, body(): pl.pallas_call(functools.partial(kernel, n_gx, n_gy), out_shape=(shape, s...  97.9 us
    unnamed x3, local copies, waits for them, and re-layouts  4.85 us

profile of v1, /device:TPU:0, one launch (start us, length us, event | category | flops | bytes accessed | tf_op | source)
XLA Modules:
  0.0 103.4 jit_solution(5275234099943341120)
XLA Ops:
  0.6 1.6 %copy.13.couple = f32[25,9,8]{2,1,0:T(8,128)} copy(f32[25,9,8]{0,2,1:T(8,128)} %param.19) | data formatting | bytes 14400 | tf_op args[8]
  2.2 97.9 %gmres.1 = (f32[3,4,16,256]{3,2,1,0:T(8,128)}, f32[3,4,16,256]{3,2,1,0:T(8,128)}) custom-call(f32[3,4,16,256]{3,2,1,0:T(8,128)} %rhs.1, f32[9,4,16,256]{3,2,1,0:T(8,128)} %diag.1, f32[6,9,4,16,256]{4,3,2,1,0:T(8,128)} %off_hbm.1, f32[9,4,16,256]{3,2,1,0:T(8,128)} %cinv_hbm.1, s32[1,3200]{1,0:T(1,128)} %send.1, s32[8,400]{1,0:T(8,128)} %recv.1, s32[8]{0:T(128)} %seg_count.1, ...), custom_call_target="tpu_custom_call" | custom-call | tf_op jit(solution)/shard_map/gmres/pallas_call | solution.py:716
  100.2 1.6 %copy.16 = f32[3,4,16,256]{3,2,1,0:T(8,128)} copy(f32[3,4,16,256]{3,2,1,0:T(8,128)} %get-tuple-element.4) | data formatting | bytes 393216
  101.8 1.6 %copy.17 = f32[3,4,16,256]{3,2,1,0:T(8,128)} copy(f32[3,4,16,256]{3,2,1,0:T(8,128)} %get-tuple-element.5) | data formatting | bytes 393216

commit v2 on v1

v2 whole, which is shorter than its diff:
```python
import functools

import jax
import jax.numpy as jnp
from jax import lax
from jax.experimental import pallas as pl
from jax.experimental.pallas import tpu as pltpu
from jax.sharding import PartitionSpec as P

CX, CY, CZ = 4, 16, 256
WELLS = 8
MAXSEG = 400
SPAN = 16
NCHUNK = 25
WIDTH = 3 * SPAN
LANES = WELLS * WIDTH
ROWS = 25
MESH = pl.DeviceIdType.MESH
F32, BF16, I32 = jnp.float32, jnp.bfloat16, jnp.int32
NEAR = [(a, b) for a in (-1, 0, 1) for b in (-1, 0, 1)]
ORDER = [7, 1, 3, 5, 6, 8, 0, 2]


def lane_pick(row, lane):
    numbers = lax.GatherDimensionNumbers(
        offset_dims=(),
        collapsed_slice_dims=(1,),
        start_index_map=(1,),
        operand_batching_dims=(0,),
        start_indices_batching_dims=(0,),
    )
    return lax.gather(
        jnp.broadcast_to(row, lane.shape),
        lane[..., None],
        numbers,
        slice_sizes=(1, 1),
        mode=lax.GatherScatterMode.PROMISE_IN_BOUNDS,
    )


def look_up(rows, lane, count, match, parts=4):
    totals = []
    for a in range(3):
        totals.append([None] * parts)
    for r in range(count):
        hit = match(r)
        for a in range(3):
            old = totals[a][r % parts]
            old = jnp.zeros(lane.shape, F32) if old is None else old
            totals[a][r % parts] = jnp.where(hit, lane_pick(rows(a, r), lane), old)
    return [functools.reduce(jnp.add, [t for t in totals[a] if t is not None]) for a in range(3)]


def kernel(
    n_gx,
    n_gy,
    rhs,
    diag,
    off_hbm,
    cinv_hbm,
    send,
    recv,
    seg_count,
    ginv_hbm,
    couple,
    sol,
    res,
    off,
    cinv,
    ginv,
    field,
    u,
    zp,
    ystage,
    yhalo,
    pool,
    slots,
    back,
    ret,
    cell,
    seg_row,
    seg_lane,
    inv_row,
    inv_lane,
    cell_row,
    cell_lane,
    spread,
    y0,
    yp,
    chain,
    ends,
    ytab,
    cpad,
    ar1,
    ar2,
    sums,
    load_sem,
    fwd_send,
    fwd_recv,
    back_send,
    back_recv,
    halo_send,
    halo_recv,
    ar1_send,
    ar1_recv,
    ar2_send,
    ar2_recv,
):
    ix = lax.axis_index("gx")
    iy = lax.axis_index("gy")
    core = lax.rem(ix, 2)
    chip = lax.div(ix, 2)
    chips = n_gx // 2
    near = 2 * n_gy

    loads = [
        pltpu.make_async_copy(cinv_hbm, cinv, load_sem.at[0]),
        pltpu.make_async_copy(off_hbm, off, load_sem.at[1]),
    ] + [
        pltpu.make_async_copy(
            ginv_hbm.at[:, j * 128 : j * 128 + 128], ginv.at[j], load_sem.at[2 + j]
        )
        for j in range(3)
    ]
    for load in loads:
        load.start()

    def exists(q):
        a, b = NEAR[q]
        good = True
        if a < 0:
            good = ix > 0
        elif a > 0:
            good = ix < n_gx - 1
        if b < 0:
            good = good & (iy > 0)
        elif b > 0:
            good = good & (iy < n_gy - 1)
        return good

    def device(q):
        if isinstance(q, int):
            return (ix + NEAR[q][0], iy + NEAR[q][1])
        return (ix + lax.div(q, 3) - 1, iy + lax.rem(q, 3) - 1)

    def exists_at(q):
        gx, gy = device(q)
        return (gx >= 0) & (gx < n_gx) & (gy >= 0) & (gy < n_gy) & (q != 4)

    def near_device(d):
        place = lax.rem(core * n_gy + iy + d, near)
        return (chip * 2 + lax.div(place, n_gy), lax.rem(place, n_gy))

    def far_device(d):
        return (lax.rem(chip + d, chips) * 2 + core, iy)

    barrier = pltpu.get_barrier_semaphore()
    for q in ORDER:

        @pl.when(exists(q))
        def _(q=q):
            pl.semaphore_signal(barrier, inc=1, device_id=device(q), device_id_type=MESH)

    for d in range(1, near):
        pl.semaphore_signal(barrier, inc=1, device_id=near_device(d), device_id_type=MESH)
    for d in range(1, chips):
        pl.semaphore_signal(barrier, inc=1, device_id=far_device(d), device_id_type=MESH)

    def present(edge):
        return jnp.where(edge, 1, 0)

    across_x = 1 + present(ix > 0) + present(ix < n_gx - 1)
    across_y = 1 + present(iy > 0) + present(iy < n_gy - 1)
    greeted = across_x * across_y - 1 + (near - 1) + (chips - 1)

    def fwd_copy(it, q):
        return pltpu.make_async_remote_copy(
            src_ref=pool.at[it, 4],
            dst_ref=pool.at[it, 8 - q],
            send_sem=fwd_send.at[it, q],
            recv_sem=fwd_recv.at[it, 8 - q],
            device_id=device(q),
            device_id_type=MESH,
        )

    def fwd_arrival(it, q):
        return pltpu.make_async_remote_copy(
            src_ref=pool.at[it, 4],
            dst_ref=pool.at[it, q],
            send_sem=fwd_send.at[it, 8 - q],
            recv_sem=fwd_recv.at[it, q],
            device_id=device(q),
            device_id_type=MESH,
        )

    def back_copy(it, q):
        return pltpu.make_async_remote_copy(
            src_ref=slots.at[it, q],
            dst_ref=back.at[it, 8 - q],
            send_sem=back_send.at[it, q],
            recv_sem=back_recv.at[it, 8 - q],
            device_id=device(q),
            device_id_type=MESH,
        )

    side_place = [1, 7, 3, 5]

    def halo_copy(it, side):
        if side < 2:
            src = zp.at[it, 1 if side == 0 else CX]
            dst = zp.at[it, CX + 1 if side == 0 else 0]
        else:
            src = ystage.at[it, side - 2]
            dst = yhalo.at[it, 3 - side]
        other = side ^ 1
        return pltpu.make_async_remote_copy(
            src_ref=src,
            dst_ref=dst,
            send_sem=halo_send.at[it, side],
            recv_sem=halo_recv.at[it, other],
            device_id=device(side_place[side]),
            device_id_type=MESH,
        )

    def near_copy(i, d):
        return pltpu.make_async_remote_copy(
            src_ref=ar1.at[i, 0],
            dst_ref=ar1.at[i, d],
            send_sem=ar1_send.at[i, d],
            recv_sem=ar1_recv.at[i, d],
            device_id=near_device(d),
            device_id_type=MESH,
        )

    def far_copy(i, d):
        return pltpu.make_async_remote_copy(
            src_ref=ar2.at[i, 0],
            dst_ref=ar2.at[i, d],
            send_sem=ar2_send.at[i, d],
            recv_sem=ar2_recv.at[i, d],
            device_id=far_device(d),
            device_id_type=MESH,
        )

    def sent(it, copy, count, place=lambda k: k):
        for k in range(count):
            if place(k) != 4:

                @pl.when(exists(place(k)))
                def _(k=k):
                    copy(it, k).wait_send()

    def sent_halo(it):
        sent(it, halo_copy, 4, lambda side: side_place[side])

    def sent_sums(i):
        for d in range(1, near):
            near_copy(i, d).wait_send()
        for d in range(1, chips):
            far_copy(i, d).wait_send()

    def send_near(i):
        for d in range(1, near):
            near_copy(i, d).start()

    def pass_on(i):
        total = ar1[i, 0]
        for d in range(1, near):
            near_copy(i, d).wait_recv()
            total = total + ar1[i, d]
        ar2[i, 0] = total
        for d in range(1, chips):
            far_copy(i, d).start()

    def collect(i):
        total = ar2[i, 0]
        for d in range(1, chips):
            far_copy(i, d).wait_recv()
            total = total + ar2[i, d]
        return total

    for c in range(ROWS):
        cell[c : c + 1, :] = send[:, c * 128 : (c + 1) * 128]

    field[0] = rhs[...]

    def forward(it):
        for a in range(3):
            total = diag[3 * a] * field[it, 0]
            total = total + diag[3 * a + 1] * field[it, 1]
            total = total + diag[3 * a + 2] * field[it, 2]
            u[a, 0] = total[:, :, :128]
            u[a, 1] = total[:, :, 128:]
        where = cell[...]
        high = where >> 7
        lane = where & 127
        sub = lax.broadcasted_iota(I32, (8, 128), 0)
        tiles = [slice(8 * i, 8 * i + 8) for i in range(3)]
        end_high = jnp.broadcast_to(high[24:25], (8, 128)) - 2 * sub
        end_lane = jnp.broadcast_to(lane[24:25], (8, 128))

        def step(g, got):
            got = list(got)
            for i, tile in enumerate(tiles):
                base = high[tile] - 64 * g
                new = look_up(
                    lambda a, r: u[a, r % 2, 2 * g + r // 32, r // 2 % 16 : r // 2 % 16 + 1, :],
                    lane[tile],
                    64,
                    lambda r: base == r,
                )
                for a in range(3):
                    got[3 * i + a] = got[3 * i + a] + new[a]
            base = end_high - 64 * g
            for r in range(0, 32, 8):
                for half in range(2):
                    match = base == 2 * r + half
                    for a in range(3):
                        here = u[a, half, 2 * g + r // 16, r % 16 : r % 16 + 8, :]
                        value = lane_pick(here, end_lane)
                        got[9 + a] = jnp.where(match, value, got[9 + a])
            return tuple(got)

        none = jnp.zeros((8, 128), F32)
        got = lax.fori_loop(0, CX // 2, step, tuple([none] * 12))
        for a in range(3):
            for i, tile in enumerate(tiles):
                pool[it, 4, a, tile] = got[3 * i + a]
            pool[it, 4, a, 24:25] = jnp.sum(got[9 + a], axis=0, keepdims=True)

    def send_forward(it):
        for q in ORDER:

            @pl.when(exists(q))
            def _(q=q):
                fwd_copy(it, q).start()

    def setup():
        total = jnp.zeros((CX * CY, 2 * CZ), F32)
        for start, width in ((0, 1024), (1024, 1024), (2048, 1024), (3072, 128)):
            where = send[:, start : start + width]
            slot = lax.broadcasted_iota(I32, (1, width), 1) + start
            left = lax.broadcasted_iota(I32, (CX * CY, width), 0) == (where >> 8)
            hit = lax.broadcasted_iota(I32, (CZ, width), 0) == (where & 255)
            row = jnp.where(hit, ((slot >> 7) + 1).astype(F32), 0.0)
            lane = jnp.where(hit, (slot & 127).astype(F32), 0.0)
            total = total + lax.dot_general(
                jnp.where(left, 1.0, 0.0).astype(BF16),
                jnp.concatenate([row, lane], axis=0).astype(BF16),
                (((1,), (1,)), ((), ())),
                preferred_element_type=F32,
            )
        cell_row[...] = total[:, :CZ].astype(I32).reshape(CX, CY, CZ) - 1
        cell_lane[...] = total[:, CZ:].astype(I32).reshape(CX, CY, CZ)

        seg_lane[...] = jnp.zeros(seg_lane.shape, I32)
        seg_lane[:, :MAXSEG] = recv[...]
        position = seg_lane[...]
        well = lax.broadcasted_iota(I32, (WELLS, 512), 0)
        segment = lax.broadcasted_iota(I32, (WELLS, 512), 1)
        count = jnp.zeros((WELLS, 512), I32)
        for w in range(WELLS):
            count = jnp.where(well == w, seg_count[w], count)
        live = (segment < count) & (segment < MAXSEG)
        high = position >> 7
        seg_row[...] = jnp.where(live, high, -1)
        seg_lane[...] = position & 127

        sub232 = lax.broadcasted_iota(I32, (232, 512), 0)
        sub128 = lax.broadcasted_iota(I32, (128, 512), 0)
        along = lax.broadcasted_iota(I32, (1, 512), 1)
        total = jnp.zeros((232, 256), F32)
        for w in range(WELLS):
            high = seg_row[w : w + 1, :]
            slab = (high * 1311) >> 15
            row_in = high - ROWS * slab
            goal = jnp.where(row_in == ROWS - 1, 9 * 24 + slab, 24 * slab + row_in)
            left = sub232 == jnp.where(high < 0, -1, goal)
            hit = sub128 == seg_lane[w : w + 1, :]
            row = jnp.where(hit, ((along >> 4) + 1).astype(F32), 0.0)
            lane = jnp.where(hit, ((along & 15) + w * SPAN).astype(F32), 0.0)
            total = total + lax.dot_general(
                jnp.where(left, 1.0, 0.0).astype(BF16),
                jnp.concatenate([row, lane], axis=0).astype(BF16),
                (((1,), (1,)), ((), ())),
                preferred_element_type=F32,
            )
        for q in range(9):
            inv_row[q] = total[24 * q : 24 * q + 24, :128].astype(I32) - 1
            inv_lane[q] = total[24 * q : 24 * q + 24, 128:].astype(I32)
        inv_row[9, 0:16] = total[216:232, :128].astype(I32) - 1
        inv_lane[9, 0:16] = total[216:232, 128:].astype(I32)

        for j in range(3):
            loads[2 + j].wait()
        y0[...] = jnp.zeros(y0.shape, F32)
        group = lax.broadcasted_iota(I32, (32, 128), 1) >> 4
        firsts = []
        for k in range(3):
            for j in range(3):
                y0[j, 0:NCHUNK] = ginv[j, pl.ds(k, NCHUNK, stride=WIDTH), :]
            firsts.append(permuted())
        pairs = []
        cpad[...] = jnp.zeros(cpad.shape, F32)
        for kb in range(9):
            cpad[0:WELLS, 0:NCHUNK] = couple[kb]
            pairs.append(lane_pick(cpad[...].T[0:32], group)[:NCHUNK])
        for a in range(3):
            for b in range(3):
                total = firsts[0][a][:NCHUNK] * pairs[b]
                for k in (1, 2):
                    total = total + firsts[k][a][:NCHUNK] * pairs[3 * k + b]
                chain[3 * a + b] = total
        for b in range(3):
            ends[b, 0:8] = jnp.zeros((8, 128), F32)

    def permuted():
        lane = lax.broadcasted_iota(I32, (8, 128), 1)
        result = []
        for a in range(3):
            source = (lane >> 4) * WIDTH + 3 * (lane & 15) + a
            tiles = [None] * 4
            for j in range(3):
                here = (source >> 7) == j
                for i in range(4):
                    value = lane_pick(y0[j, 8 * i : 8 * i + 8], source & 127)
                    tiles[i] = value if j == 0 else jnp.where(here, value, tiles[i])
            result.append(jnp.concatenate(tiles, axis=0))
        return result

    def wells(it):
        row_of = seg_row[...]
        lane_of = seg_lane[...]
        tiles = [slice(128 * i, 128 * i + 128) for i in range(3)]
        sub = lax.broadcasted_iota(I32, (8, 128), 0)
        along = lax.broadcasted_iota(I32, (8, 128), 1)
        mine = (along >> 4) == sub

        def one_row(values):
            value = lane_pick(values[:, 384:], along & 15)
            return jnp.sum(jnp.where(mine, value, 0), axis=0, keepdims=True)

        end_row = jnp.broadcast_to(one_row(row_of), (8, 128)) - sub
        end_lane = jnp.broadcast_to(one_row(lane_of), (8, 128))

        def take(q, got):
            got = list(got)
            for i, tile in enumerate(tiles):
                base = row_of[:, tile] - q * ROWS
                new = look_up(
                    lambda a, r: pool[it, q, a, r : r + 1, :],
                    lane_of[:, tile],
                    ROWS,
                    lambda r: base == r,
                )
                for a in range(3):
                    got[3 * i + a] = got[3 * i + a] + new[a]
            base = end_row - q * ROWS
            for r in range(0, 24, 8):
                match = base == r
                for a in range(3):
                    value = lane_pick(pool[it, q, a, r : r + 8, :], end_lane)
                    got[9 + a] = jnp.where(match, value, got[9 + a])
            match = (base == 24) & (sub == 0)
            for a in range(3):
                value = lane_pick(pool[it, q, a, 24:25, :], end_lane)
                got[9 + a] = jnp.where(match, value, got[9 + a])
            return tuple(got)

        def step(p, got):
            q = lax.rem(2 * p + 1, 5)
            for side in (q, 8 - q):

                @pl.when(exists_at(side))
                def _(side=side):
                    fwd_arrival(it, side).wait_recv()

            return take(8 - q, take(q, got))

        none = jnp.zeros((WELLS, 128), F32)
        got = take(4, tuple([none] * 12))
        got = list(lax.fori_loop(0, 4, step, got))
        for a in range(3):
            value = jnp.sum(got[9 + a], axis=0, keepdims=True)
            value = lane_pick(value, (sub * 16 + along) & 127)
            got[9 + a] = jnp.where(along < 16, value, 0.0)
        none = jnp.zeros((WELLS, 128), F32)
        for i in range(4):
            square = jnp.concatenate([got[3 * i + a] for a in range(3)] + [none] * 13, axis=0)
            spread[128 * i : 128 * i + 128] = square.T
        well = [(along + 128 * j) // WIDTH for j in range(3)]
        for j in range(3):
            totals = [None] * NCHUNK
            for a in range(3):
                for c in range(NCHUNK):
                    for at in (SPAN * c, SPAN * c + 8):
                        r = lane_pick(spread[at : at + 8], well[j] + 8 * a)
                        g = ginv[j, pl.ds(3 * at + a, 8, stride=3), :]
                        totals[c] = g * r if totals[c] is None else totals[c] + g * r
            for c in range(NCHUNK):
                y0[j, c : c + 1, :] = jnp.sum(totals[c], axis=0, keepdims=True)
        moved = permuted()
        for a in range(3):
            yp[a] = moved[a]

        def link(c, last):
            new = []
            for a in range(3):
                value = yp[a, pl.ds(c, 1), :]
                for b in range(3):
                    value = value - chain[3 * a + b, pl.ds(c, 1), :] * last[b]
                new.append(value)
            for a in range(3):
                ends[a, pl.ds(c + 1, 1), :] = new[a]
            return tuple(new)

        lax.fori_loop(0, NCHUNK, link, tuple([jnp.zeros((1, 128), F32)] * 3), unroll=5)
        last_lane = lax.broadcasted_iota(I32, (NCHUNK, 128), 1) | 15
        before = [lane_pick(ends[b, 0:NCHUNK, :], last_lane) for b in range(3)]
        for a in range(3):
            value = yp[a, 0:NCHUNK]
            for b in range(3):
                value = value - chain[3 * a + b] * before[b]
            ytab[a] = value

        def corrections(row_at, lane_at):
            return look_up(
                lambda a, r: ytab[a, r : r + 1, :], lane_at, ROWS, lambda r: row_at == r
            )

        for half in range(2):
            tile = slice(8 * half, 8 * half + 8)
            got = corrections(inv_row[9, tile], inv_lane[9, tile])
            for q in range(8 * half, min(9, 8 * half + 8)):
                for a in range(3):
                    slots[it, q, a, 24:25] = got[a][q - 8 * half : q - 8 * half + 1]

        def give(q):
            for i in range(3):
                tile = slice(8 * i, 8 * i + 8)
                got = corrections(inv_row[q, tile], inv_lane[q, tile])
                for a in range(3):
                    slots[it, q, a, tile] = got[a]

        def give_pair(t, carry):
            q = lax.rem(2 * (3 - t) + 1, 5)
            give(q)
            give(8 - q)
            for side in (q, 8 - q):

                @pl.when(exists_at(side))
                def _(side=side):
                    back_copy(it, side).start()

            return carry

        lax.fori_loop(0, 4, give_pair, 0)
        give(4)

    def backward(it):
        ret[...] = slots[it, 4]
        for q in ORDER:

            @pl.when(exists(q))
            def _(q=q):
                back_copy(it, 8 - q).wait_recv()
                ret[...] = ret[...] + back[it, q]

        def plane(x):
            for i in range(2):
                sides = []
                for half in range(2):
                    tile = (slice(8 * i, 8 * i + 8), slice(128 * half, 128 * half + 128))
                    row_at = cell_row[(x,) + tile]
                    lane_at = cell_lane[(x,) + tile]
                    got = look_up(
                        lambda a, r: ret[a, r : r + 1, :], lane_at, ROWS, lambda r: row_at == r
                    )
                    for a in range(3):
                        value = got[a]
                        for b in range(3):
                            value = value + cinv[(3 * a + b, x) + tile] * field[(it, b, x) + tile]
                        zp[(it, x + 1, a) + tile] = value
                        if i == 0:
                            ystage[it, 0, x, a : a + 1, tile[1]] = value[0:1]
                        else:
                            ystage[it, 1, x, a : a + 1, tile[1]] = value[7:8]

        def planes(t, carry):
            plane(t)
            plane(3 - t)

            @pl.when((t == 0) & exists(1))
            def _():
                halo_copy(it, 0).start()

            @pl.when((t == 0) & exists(7))
            def _():
                halo_copy(it, 1).start()

            return carry

        lax.fori_loop(0, 2, planes, 0)
        start_halo(it, 2)
        start_halo(it, 3)

    def start_halo(it, side):
        @pl.when(exists(side_place[side]))
        def _():
            halo_copy(it, side).start()

    def jacobian(it, between=lambda: None):
        row = lax.broadcasted_iota(I32, (CY, CZ), 0)
        column = lax.broadcasted_iota(I32, (CY, CZ), 1)
        for x in range(CX):
            total = [None] * 3

            def add(blocks, value, b):
                for a in range(3):
                    term = blocks(3 * a + b) * value
                    total[a] = term if total[a] is None else total[a] + term

            for b in range(3):
                here = zp[it, x + 1, b]
                add(lambda e: diag[e, x], here, b)
                if x > 0:
                    add(lambda e: off[0, e, x], zp[it, x, b], b)
                if x < CX - 1:
                    add(lambda e: off[1, e, x], zp[it, x + 2, b], b)
                value = jnp.where(row > 0, pltpu.roll(here, 1, 0), 0.0)
                add(lambda e: off[2, e, x], value, b)
                value = jnp.where(row < CY - 1, pltpu.roll(here, CY - 1, 0), 0.0)
                add(lambda e: off[3, e, x], value, b)
                value = jnp.where(column > 0, pltpu.roll(here, 1, 1), 0.0)
                add(lambda e: off[4, e, x], value, b)
                value = jnp.where(column < CZ - 1, pltpu.roll(here, CZ - 1, 1), 0.0)
                add(lambda e: off[5, e, x], value, b)
            for a in range(3):
                field[it + 1, a, x] = total[a]

        result = between()
        for side in range(4):

            @pl.when(exists(side_place[side]))
            def _(side=side):
                halo_copy(it, side ^ 1).wait_recv()
                if side < 2:
                    x = 0 if side == 0 else CX - 1
                    plane = 0 if side == 0 else CX + 1
                    for a in range(3):
                        value = field[it + 1, a, x]
                        for b in range(3):
                            value = value + off[side, 3 * a + b, x] * zp[it, plane, b]
                        field[it + 1, a, x] = value
                else:
                    y = 0 if side == 2 else CY - 1
                    for x in range(CX):
                        for a in range(3):
                            value = field[it + 1, a, x, y : y + 1, :]
                            for b in range(3):
                                beside = yhalo[it, side - 2, x, b : b + 1, :]
                                value = value + off[side, 3 * a + b, x, y : y + 1, :] * beside
                            field[it + 1, a, x, y : y + 1, :] = value
        return result

    def dot_row(place, first, second):
        total = None
        for a in range(3):
            for x in range(CX):
                product = first(a, x) * second(a, x)
                total = product if total is None else total + product
        total = jnp.sum(total, axis=0, keepdims=True)
        sums[place : place + 1, :] = total[:, :128] + total[:, 128:]

    def pack_sums(i):
        sub = lax.broadcasted_iota(I32, (8, 128), 0)
        along = lax.broadcasted_iota(I32, (8, 128), 1)
        total = jnp.sum(sums[...], axis=1, keepdims=True)
        ar1[i, 0] = jnp.sum(jnp.where(sub == along, total, 0.0), axis=0, keepdims=True)

    sums[...] = jnp.zeros((8, 128), F32)

    r_of = lambda a, x: rhs[a, x]
    w1_of = lambda a, x: field[1, a, x]
    w2_of = lambda a, x: field[2, a, x]
    v2_of = lambda a, x: field[0, a, x]

    forward(0)
    pl.semaphore_wait(barrier, greeted)
    send_forward(0)
    setup()
    wells(0)
    sent(0, fwd_copy, 9)
    loads[0].wait()
    backward(0)
    loads[1].wait()
    jacobian(0)
    forward(1)
    send_forward(1)
    dot_row(0, r_of, r_of)
    dot_row(1, w1_of, r_of)
    pack_sums(0)
    send_near(0)
    sent(0, back_copy, 9)
    sent_halo(0)
    wells(1)
    pass_on(0)
    sent(1, fwd_copy, 9)
    backward(1)

    def between():
        first = collect(0)
        square = first[:, 0:1]
        along = first[:, 1:2] / square
        for a in range(3):
            for x in range(CX):
                field[0, a, x] = field[1, a, x] - along * rhs[a, x]
        dot_row(0, v2_of, v2_of)
        dot_row(4, v2_of, r_of)
        return square, along

    square, along = jacobian(1, between)
    for a in range(3):
        for x in range(CX):
            field[2, a, x] = field[2, a, x] - along * field[1, a, x]
    dot_row(1, w2_of, r_of)
    dot_row(2, w2_of, v2_of)
    dot_row(3, w2_of, w2_of)
    pack_sums(1)
    send_near(1)
    sent(1, back_copy, 9)
    sent_halo(1)
    sent_sums(0)
    pass_on(1)
    second = collect(1)

    beta = jnp.sqrt(square)
    size = jnp.sqrt(second[:, 0:1])
    top_first = along
    sub_first = size / beta
    top_second = second[:, 1:2] / (size * beta)
    mid_second = second[:, 2:3] / (size * size) - top_second * (second[:, 4:5] / (size * beta))
    gram_first = top_first * top_first + sub_first * sub_first
    gram_cross = top_first * top_second + sub_first * mid_second
    gram_second = second[:, 3:4] / (size * size)
    determinant = gram_first * gram_second - gram_cross * gram_cross
    weight_one = (gram_second * beta * top_first - gram_cross * beta * top_second) / determinant
    weight_two = (gram_first * beta * top_second - gram_cross * beta * top_first) / determinant
    one = weight_one / beta
    two = weight_two / size
    mixed = one - two * along
    for a in range(3):
        for x in range(CX):
            sol[a, x] = mixed * zp[0, x + 1, a] + two * zp[1, x + 1, a]
            res[a, x] = rhs[a, x] - one * field[1, a, x] - two * field[2, a, x]
    sent_sums(1)


def body(
    right_side,
    diag_blocks,
    off_blocks,
    cell_inverse,
    send_cells,
    recv_index,
    seg_count,
    span_inverse,
    span_couple,
):
    n_gx, n_gy = lax.axis_size("gx"), lax.axis_size("gy")
    vmem = pl.BlockSpec(memory_space=pltpu.VMEM)
    anywhere = pl.BlockSpec(memory_space=pl.ANY)
    smem = pl.BlockSpec(memory_space=pltpu.SMEM)
    shape = jax.ShapeDtypeStruct(right_side.shape, F32)
    dma = pltpu.SemaphoreType.DMA
    scratch = [
        pltpu.VMEM((6, 9, CX, CY, CZ), F32),
        pltpu.VMEM((9, CX, CY, CZ), F32),
        pltpu.VMEM((3, NCHUNK * WIDTH, 128), F32),
        pltpu.VMEM((3, 3, CX, CY, CZ), F32),
        pltpu.VMEM((3, 2, CX, CY, 128), F32),
        pltpu.VMEM((2, CX + 2, 3, CY, CZ), F32),
        pltpu.VMEM((2, 2, CX, 3, CZ), F32),
        pltpu.VMEM((2, 2, CX, 3, CZ), F32),
        pltpu.VMEM((2, 9, 3, ROWS, 128), F32),
        pltpu.VMEM((2, 9, 3, ROWS, 128), F32),
        pltpu.VMEM((2, 9, 3, ROWS, 128), F32),
        pltpu.VMEM((3, ROWS, 128), F32),
        pltpu.VMEM((ROWS, 128), I32),
        pltpu.VMEM((WELLS, 512), I32),
        pltpu.VMEM((WELLS, 512), I32),
        pltpu.VMEM((10, 24, 128), I32),
        pltpu.VMEM((10, 24, 128), I32),
        pltpu.VMEM((CX, CY, CZ), I32),
        pltpu.VMEM((CX, CY, CZ), I32),
        pltpu.VMEM((512, 128), F32),
        pltpu.VMEM((3, 32, 128), F32),
        pltpu.VMEM((3, 32, 128), F32),
        pltpu.VMEM((9, NCHUNK, 128), F32),
        pltpu.VMEM((3, 32, 128), F32),
        pltpu.VMEM((3, NCHUNK, 128), F32),
        pltpu.VMEM((128, 128), F32),
        pltpu.VMEM((2, 2 * n_gy, 1, 128), F32),
        pltpu.VMEM((2, n_gx // 2, 1, 128), F32),
        pltpu.VMEM((8, 128), F32),
        dma((5,)),
        dma((2, 9)),
        dma((2, 9)),
        dma((2, 9)),
        dma((2, 9)),
        dma((2, 4)),
        dma((2, 4)),
        dma((2, 2 * n_gy)),
        dma((2, 2 * n_gy)),
        dma((2, n_gx // 2)),
        dma((2, n_gx // 2)),
    ]
    return pl.pallas_call(
        functools.partial(kernel, n_gx, n_gy),
        out_shape=(shape, shape),
        in_specs=[vmem, vmem, anywhere, anywhere, vmem, vmem, smem, anywhere, vmem],
        out_specs=(vmem, vmem),
        scratch_shapes=scratch,
        compiler_params=pltpu.CompilerParams(collective_id=0, has_side_effects=True),
        name="gmres",
    )(
        right_side,
        diag_blocks,
        off_blocks,
        cell_inverse,
        send_cells,
        recv_index,
        seg_count,
        span_inverse.reshape(NCHUNK * WIDTH, LANES),
        span_couple.transpose(1, 2, 0),
    )


def solution(mesh):
    return jax.shard_map(
        body,
        mesh=mesh,
        in_specs=(
            P(None, "gx", "gy", None),
            P(None, "gx", "gy", None),
            P(None, None, "gx", "gy", None),
            P(None, "gx", "gy", None),
            P(("gx", "gy"), None),
            P(("gx", "gy"), None),
            P(("gx", "gy")),
            P(None, None, ("gx", "gy")),
            P(None, None, ("gx", "gy")),
        ),
        out_specs=(P(None, "gx", "gy", None), P(None, "gx", "gy", None)),
        check_vma=False,
    )
```

time: 104 us -> 61.7 us (0.59)
  Pallas kernels: 97.9 us -> 57.7 us
  local copies, waits for them, and re-layouts: 4.85 us -> 3.23 us
    pallas_call x1, Pallas kernels: 97.9 us -> 57.7 us  [body(): pl.pallas_call(functools.partial(kernel, n_gx, n_gy), out_shape=(shape, s...]
    unnamed x3 -> x2, local copies, waits for them, and re-layouts: 4.85 us -> 3.23 us
where the time goes in v2:
time: 61.7 us; the launch traced here: 61.6 us
  Pallas kernels  57.7 us (94%)
  local copies, waits for them, and re-layouts  3.23 us (5%)
  between operations  0.64 us (1%)
    pallas_call x1, Pallas kernels, body(): pl.pallas_call(functools.partial(kernel, n_gx, n_gy), out_shape=(shape, s...  57.7 us
    unnamed x2, local copies, waits for them, and re-layouts  3.23 us

profile of v2, /device:TPU:0, one launch (start us, length us, event | category | flops | bytes accessed | tf_op | source)
XLA Modules:
  0.0 61.6 jit_solution(16586615786640808394)
XLA Ops:
  0.6 57.7 %gmres.1 = (f32[3,4,16,256]{3,2,1,0:T(8,128)}, f32[3,4,16,256]{3,2,1,0:T(8,128)}) custom-call(f32[3,4,16,256]{3,2,1,0:T(8,128)} %rhs.1, f32[9,4,16,256]{3,2,1,0:T(8,128)} %diag.1, f32[6,9,4,16,256]{4,3,2,1,0:T(8,128)} %off_hbm.1, f32[9,4,16,256]{3,2,1,0:T(8,128)} %cinv_hbm.1, s32[1,3200]{1,0:T(1,128)} %send.1, s32[8,400]{1,0:T(8,128)} %recv.1, s32[8]{0:T(128)} %seg_count.1, ...), custom_call_target="tpu_custom_call" | custom-call | tf_op jit(solution)/shard_map/gmres/pallas_call | solution.py:818
  58.3 1.6 %copy.13 = f32[3,4,16,256]{3,2,1,0:T(8,128)} copy(f32[3,4,16,256]{3,2,1,0:T(8,128)} %get-tuple-element.4) | data formatting | bytes 393216
  59.9 1.6 %copy.14 = f32[3,4,16,256]{3,2,1,0:T(8,128)} copy(f32[3,4,16,256]{3,2,1,0:T(8,128)} %get-tuple-element.5) | data formatting | bytes 393216

commit v3 on v2

--- a/solution.py
+++ b/solution.py
@@ -38,17 +38,22 @@
     )
 
 
-def look_up(rows, lane, count, match, parts=4):
-    totals = []
-    for a in range(3):
-        totals.append([None] * parts)
-    for r in range(count):
-        hit = match(r)
-        for a in range(3):
-            old = totals[a][r % parts]
-            old = jnp.zeros(lane.shape, F32) if old is None else old
-            totals[a][r % parts] = jnp.where(hit, lane_pick(rows(a, r), lane), old)
-    return [functools.reduce(jnp.add, [t for t in totals[a] if t is not None]) for a in range(3)]
+def look_up(rows, lane, count, row_at, old=None):
+    levels = (count - 1).bit_length()
+    bits = [(row_at & (1 << b)) != 0 for b in range(levels)]
+    inside = (row_at >= 0) & (row_at < count)
+
+    def tree(a, low, level):
+        if level == 0:
+            return lane_pick(rows(a, low), lane)
+        left = tree(a, low, level - 1)
+        if low + (1 << level - 1) >= count:
+            return left
+        return jnp.where(bits[level - 1], tree(a, low + (1 << level - 1), level - 1), left)
+
+    return [
+        jnp.where(inside, tree(a, 0, levels), 0.0 if old is None else old[a]) for a in range(3)
+    ]
 
 
 def kernel(
@@ -76,6 +81,7 @@
     pool,
     slots,
     back,
+    relay,
     ret,
     cell,
     seg_row,
@@ -99,6 +105,7 @@
     fwd_recv,
     back_send,
     back_recv,
+    relay_recv,
     halo_send,
     halo_recv,
     ar1_send,
@@ -147,6 +154,17 @@
         gx, gy = device(q)
         return (gx >= 0) & (gx < n_gx) & (gy >= 0) & (gy < n_gy) & (q != 4)
 
+    partner = 1 - 2 * core
+
+    def direct(q):
+        a, b = NEAR[q]
+        return exists(q) & (partner != a) if a and b else exists(q)
+
+    def pair(kind):
+        middle = 4 + 3 * partner * jnp.where(kind == 3, 1, jnp.where(kind == 2, -1, 0))
+        reach = jnp.where(kind == 1, 3, 1)
+        return (middle - reach, middle + reach)
+
     def near_device(d):
         place = lax.rem(core * n_gy + iy + d, near)
         return (chip * 2 + lax.div(place, n_gy), lax.rem(place, n_gy))
@@ -190,6 +208,28 @@
             send_sem=fwd_send.at[it, 8 - q],
             recv_sem=fwd_recv.at[it, q],
             device_id=device(q),
+            device_id_type=MESH,
+        )
+
+    def fwd_relay(it, side):
+        b = 2 * side - 1
+        return pltpu.make_async_remote_copy(
+            src_ref=pool.at[it, 4 + b],
+            dst_ref=pool.at[it, 4 - 3 * partner + b],
+            send_sem=fwd_send.at[it, 4 + 3 * partner + b],
+            recv_sem=fwd_recv.at[it, 4 - 3 * partner + b],
+            device_id=(ix + partner, iy),
+            device_id_type=MESH,
+        )
+
+    def back_relay(it, side):
+        q = 4 + 3 * partner + 2 * side - 1
+        return pltpu.make_async_remote_copy(
+            src_ref=slots.at[it, q],
+            dst_ref=relay.at[it, side],
+            send_sem=back_send.at[it, q],
+            recv_sem=relay_recv.at[it, side],
+            device_id=(ix + partner, iy),
             device_id_type=MESH,
         )
 
@@ -307,10 +347,10 @@
                     lambda a, r: u[a, r % 2, 2 * g + r // 32, r // 2 % 16 : r // 2 % 16 + 1, :],
                     lane[tile],
                     64,
-                    lambda r: base == r,
+                    base,
+                    got[3 * i : 3 * i + 3],
                 )
-                for a in range(3):
-                    got[3 * i + a] = got[3 * i + a] + new[a]
+                got[3 * i : 3 * i + 3] = new
             base = end_high - 64 * g
             for r in range(0, 32, 8):
                 for half in range(2):
@@ -331,7 +371,7 @@
     def send_forward(it):
         for q in ORDER:
 
-            @pl.when(exists(q))
+            @pl.when(direct(q))
             def _(q=q):
                 fwd_copy(it, q).start()
 
@@ -451,10 +491,10 @@
                     lambda a, r: pool[it, q, a, r : r + 1, :],
                     lane_of[:, tile],
                     ROWS,
-                    lambda r: base == r,
+                    base,
+                    got[3 * i : 3 * i + 3],
                 )
-                for a in range(3):
-                    got[3 * i + a] = got[3 * i + a] + new[a]
+                got[3 * i : 3 * i + 3] = new
             base = end_row - q * ROWS
             for r in range(0, 24, 8):
                 match = base == r
@@ -468,17 +508,24 @@
             return tuple(got)
 
         def step(p, got):
-            q = lax.rem(2 * p + 1, 5)
-            for side in (q, 8 - q):
-
-                @pl.when(exists_at(side))
+            low, high = pair(p)
+            for side in (low, high):
+
+                @pl.when(exists_at(side) & (p > 0))
                 def _(side=side):
                     fwd_arrival(it, side).wait_recv()
 
-            return take(8 - q, take(q, got))
+            return take(high, take(low, got))
 
         none = jnp.zeros((WELLS, 128), F32)
         got = take(4, tuple([none] * 12))
+        for side in range(2):
+
+            @pl.when(exists(3 + 2 * side))
+            def _(side=side):
+                fwd_arrival(it, 3 + 2 * side).wait_recv()
+                fwd_relay(it, side).start()
+
         got = list(lax.fori_loop(0, 4, step, got))
         for a in range(3):
             value = jnp.sum(got[9 + a], axis=0, keepdims=True)
@@ -524,9 +571,7 @@
             ytab[a] = value
 
         def corrections(row_at, lane_at):
-            return look_up(
-                lambda a, r: ytab[a, r : r + 1, :], lane_at, ROWS, lambda r: row_at == r
-            )
+            return look_up(lambda a, r: ytab[a, r : r + 1, :], lane_at, ROWS, row_at)
 
         for half in range(2):
             tile = slice(8 * half, 8 * half + 8)
@@ -543,14 +588,25 @@
                     slots[it, q, a, tile] = got[a]
 
         def give_pair(t, carry):
-            q = lax.rem(2 * (3 - t) + 1, 5)
-            give(q)
-            give(8 - q)
-            for side in (q, 8 - q):
-
-                @pl.when(exists_at(side))
+            kind = jnp.where(t == 2, 0, jnp.where(t == 3, 1, 3 - t))
+            for side, q in enumerate(pair(kind)):
+                give(q)
+
+            for side, q in enumerate(pair(kind)):
+
+                @pl.when(exists_at(q) & (t == 0))
                 def _(side=side):
-                    back_copy(it, side).start()
+                    back_relay(it, side).start()
+
+                @pl.when(exists_at(q) & (t == 2))
+                def _(side=side):
+                    back_relay(it, side).wait_recv()
+                    here = slots[it, 3 + 2 * side] + relay[it, side]
+                    slots[it, 3 + 2 * side] = here
+
+                @pl.when(exists_at(q) & (t > 0))
+                def _(q=q):
+                    back_copy(it, q).start()
 
             return carry
 
@@ -561,7 +617,7 @@
         ret[...] = slots[it, 4]
         for q in ORDER:
 
-            @pl.when(exists(q))
+            @pl.when(direct(q))
             def _(q=q):
                 back_copy(it, 8 - q).wait_recv()
                 ret[...] = ret[...] + back[it, q]
@@ -573,9 +629,7 @@
                     tile = (slice(8 * i, 8 * i + 8), slice(128 * half, 128 * half + 128))
                     row_at = cell_row[(x,) + tile]
                     lane_at = cell_lane[(x,) + tile]
-                    got = look_up(
-                        lambda a, r: ret[a, r : r + 1, :], lane_at, ROWS, lambda r: row_at == r
-                    )
+                    got = look_up(lambda a, r: ret[a, r : r + 1, :], lane_at, ROWS, row_at)
                     for a in range(3):
                         value = got[a]
                         for b in range(3):
@@ -785,6 +839,7 @@
         pltpu.VMEM((2, 9, 3, ROWS, 128), F32),
         pltpu.VMEM((2, 9, 3, ROWS, 128), F32),
         pltpu.VMEM((2, 9, 3, ROWS, 128), F32),
+        pltpu.VMEM((2, 2, 3, ROWS, 128), F32),
         pltpu.VMEM((3, ROWS, 128), F32),
         pltpu.VMEM((ROWS, 128), I32),
         pltpu.VMEM((WELLS, 512), I32),
@@ -808,6 +863,7 @@
         dma((2, 9)),
         dma((2, 9)),
         dma((2, 9)),
+        dma((2, 2)),
         dma((2, 4)),
         dma((2, 4)),
         dma((2, 2 * n_gy)),

time: 61.7 us -> 61 us (0.989)
  Pallas kernels: 57.7 us -> 56.9 us
    pallas_call x1, Pallas kernels: 57.7 us -> 56.9 us  [body(): pl.pallas_call(functools.partial(kernel, n_gx, n_gy), out_shape=(shape, s...]
where the time goes in v3:
time: 61 us; the launch traced here: 60.8 us
  Pallas kernels  56.9 us (93%)
  local copies, waits for them, and re-layouts  3.23 us (5%)
  between operations  0.64 us (1%)
    pallas_call x1, Pallas kernels, body(): pl.pallas_call(functools.partial(kernel, n_gx, n_gy), out_shape=(shape, s...  56.9 us
    unnamed x2, local copies, waits for them, and re-layouts  3.23 us

profile of v3, /device:TPU:0, one launch (start us, length us, event | category | flops | bytes accessed | tf_op | source)
XLA Modules:
  0.0 60.8 jit_solution(16643186979510869624)
XLA Ops:
  0.6 56.9 %gmres.1 = (f32[3,4,16,256]{3,2,1,0:T(8,128)}, f32[3,4,16,256]{3,2,1,0:T(8,128)}) custom-call(f32[3,4,16,256]{3,2,1,0:T(8,128)} %rhs.1, f32[9,4,16,256]{3,2,1,0:T(8,128)} %diag.1, f32[6,9,4,16,256]{4,3,2,1,0:T(8,128)} %off_hbm.1, f32[9,4,16,256]{3,2,1,0:T(8,128)} %cinv_hbm.1, s32[1,3200]{1,0:T(1,128)} %send.1, s32[8,400]{1,0:T(8,128)} %recv.1, s32[8]{0:T(128)} %seg_count.1, ...), custom_call_target="tpu_custom_call" | custom-call | tf_op jit(solution)/shard_map/gmres/pallas_call | solution.py:874
  57.5 1.6 %copy.13 = f32[3,4,16,256]{3,2,1,0:T(8,128)} copy(f32[3,4,16,256]{3,2,1,0:T(8,128)} %get-tuple-element.4) | data formatting | bytes 393216
  59.2 1.6 %copy.14 = f32[3,4,16,256]{3,2,1,0:T(8,128)} copy(f32[3,4,16,256]{3,2,1,0:T(8,128)} %get-tuple-element.5) | data formatting | bytes 393216

commit v4 on v3

--- a/solution.py
+++ b/solution.py
@@ -68,8 +68,9 @@
     seg_count,
     ginv_hbm,
     couple,
-    sol,
-    res,
+    z_out,
+    w_out,
+    weights,
     off,
     cinv,
     ginv,
@@ -782,6 +783,12 @@
     dot_row(3, w2_of, w2_of)
     pack_sums(1)
     send_near(1)
+    stores = [
+        pltpu.make_async_copy(zp.at[:, 1 : CX + 1], z_out, load_sem.at[0]),
+        pltpu.make_async_copy(field.at[1:3], w_out, load_sem.at[1]),
+    ]
+    for store in stores:
+        store.start()
     sent(1, back_copy, 9)
     sent_halo(1)
     sent_sums(0)
@@ -803,11 +810,19 @@
     one = weight_one / beta
     two = weight_two / size
     mixed = one - two * along
+    along_lanes = lax.broadcasted_iota(I32, (1, 128), 1)
+    weights[...] = jnp.where(along_lanes == 0, mixed, jnp.where(along_lanes == 1, two, one))
+    for store in stores:
+        store.wait()
+    sent_sums(1)
+
+
+def combine(rhs, z, w, weights, sol, res):
+    mixed, two, one = weights[:, 0:1], weights[:, 1:2], weights[:, 2:3]
     for a in range(3):
         for x in range(CX):
-            sol[a, x] = mixed * zp[0, x + 1, a] + two * zp[1, x + 1, a]
-            res[a, x] = rhs[a, x] - one * field[1, a, x] - two * field[2, a, x]
-    sent_sums(1)
+            sol[a, x] = mixed * z[0, x, a] + two * z[1, x, a]
+            res[a, x] = rhs[a, x] - one * w[0, a, x] - two * w[1, a, x]
 
 
 def body(
@@ -825,7 +840,6 @@
     vmem = pl.BlockSpec(memory_space=pltpu.VMEM)
     anywhere = pl.BlockSpec(memory_space=pl.ANY)
     smem = pl.BlockSpec(memory_space=pltpu.SMEM)
-    shape = jax.ShapeDtypeStruct(right_side.shape, F32)
     dma = pltpu.SemaphoreType.DMA
     scratch = [
         pltpu.VMEM((6, 9, CX, CY, CZ), F32),
@@ -871,11 +885,15 @@
         dma((2, n_gx // 2)),
         dma((2, n_gx // 2)),
     ]
-    return pl.pallas_call(
+    z, w, weights = pl.pallas_call(
         functools.partial(kernel, n_gx, n_gy),
-        out_shape=(shape, shape),
+        out_shape=(
+            jax.ShapeDtypeStruct((2, CX, 3, CY, CZ), F32),
+            jax.ShapeDtypeStruct((2, 3, CX, CY, CZ), F32),
+            jax.ShapeDtypeStruct((1, 128), F32),
+        ),
         in_specs=[vmem, vmem, anywhere, anywhere, vmem, vmem, smem, anywhere, vmem],
-        out_specs=(vmem, vmem),
+        out_specs=(anywhere, anywhere, vmem),
         scratch_shapes=scratch,
         compiler_params=pltpu.CompilerParams(collective_id=0, has_side_effects=True),
         name="gmres",
@@ -890,6 +908,14 @@
         span_inverse.reshape(NCHUNK * WIDTH, LANES),
         span_couple.transpose(1, 2, 0),
     )
+    shape = jax.ShapeDtypeStruct(right_side.shape, F32)
+    return pl.pallas_call(
+        combine,
+        out_shape=(shape, shape),
+        in_specs=[vmem] * 4,
+        out_specs=(vmem, vmem),
+        name="combine",
+    )(right_side, z, w, weights)
 
 
 def solution(mesh):

time: 61 us -> 59.4 us (0.974)
  local copies, waits for them, and re-layouts: 3.23 us -> 0 us
  Pallas kernels: 56.9 us -> 58.6 us
    unnamed x2 -> x0, local copies, waits for them, and re-layouts: 3.23 us -> none
    pallas_call x1 -> x2, Pallas kernels: 56.9 us -> 58.6 us  [the longest x1 56.6 us: body(): pl.pallas_call(functools.partial(kernel, n_gx, n_gy), out_shape=(jax.Shap...]
where the time goes in v4:
time: 59.4 us; the launch traced here: 59.3 us
  Pallas kernels  58.6 us (99%)
  between operations  0.64 us (1%)
    pallas_call x1, Pallas kernels, body(): pl.pallas_call(functools.partial(kernel, n_gx, n_gy), out_shape=(jax.Shap...  56.6 us
    pallas_call x1, Pallas kernels, body(): pl.pallas_call(combine, out_shape=(shape, shape), in_specs=[vmem] * 4, ou...  2.06 us

profile of v4, /device:TPU:0, one launch (start us, length us, event | category | flops | bytes accessed | tf_op | source)
XLA Modules:
  0.0 59.3 jit_solution(11680152485372716719)
XLA Ops:
  0.6 56.6 %gmres.1 = (f32[2,4,3,16,256]{4,3,2,1,0:T(8,128)}, f32[2,3,4,16,256]{4,3,2,1,0:T(8,128)}, f32[1,128]{1,0:T(1,128)}) custom-call(f32[3,4,16,256]{3,2,1,0:T(8,128)} %rhs.3, f32[9,4,16,256]{3,2,1,0:T(8,128)} %diag.1, f32[6,9,4,16,256]{4,3,2,1,0:T(8,128)} %off_hbm.1, f32[9,4,16,256]{3,2,1,0:T(8,128)} %cinv_hbm.1, s32[1,3200]{1,0:T(1,128)} %send.1, ...), custom_call_target="tpu_custom_call" | custom-call | tf_op jit(solution)/shard_map/gmres/pallas_call | solution.py:888
  57.2 2.1 %combine.1 = (f32[3,4,16,256]{3,2,1,0:T(8,128)}, f32[3,4,16,256]{3,2,1,0:T(8,128)}) custom-call(f32[3,4,16,256]{3,2,1,0:T(8,128)} %rhs.3, f32[2,4,3,16,256]{4,3,2,1,0:T(8,128)} %get-tuple-element.5.z, f32[2,3,4,16,256]{4,3,2,1,0:T(8,128)} %get-tuple-element.6.w, f32[1,128]{1,0:T(1,128)} %get-tuple-element.7.weights), custom_call_target="tpu_custom_call" | custom-call | tf_op jit(solution)/shard_map/combine/pallas_call | solution.py:912

commit v5 on v4

--- a/solution.py
+++ b/solution.py
@@ -59,15 +59,15 @@
 def kernel(
     n_gx,
     n_gy,
-    rhs,
-    diag,
+    rhs_hbm,
+    diag_hbm,
     off_hbm,
     cinv_hbm,
-    send,
-    recv,
-    seg_count,
+    send_hbm,
+    recv_hbm,
+    seg_count_hbm,
     ginv_hbm,
-    couple,
+    couple_hbm,
     z_out,
     w_out,
     weights,
@@ -101,6 +101,12 @@
     ar1,
     ar2,
     sums,
+    rhs,
+    diag,
+    send,
+    recv,
+    seg_count,
+    couple,
     load_sem,
     fwd_send,
     fwd_recv,
@@ -130,7 +136,20 @@
         )
         for j in range(3)
     ]
-    for load in loads:
+    early = [
+        pltpu.make_async_copy(source, goal, load_sem.at[5 + i])
+        for i, (source, goal) in enumerate(
+            [
+                (rhs_hbm, rhs),
+                (diag_hbm, diag),
+                (send_hbm, send),
+                (recv_hbm, recv),
+                (seg_count_hbm, seg_count),
+                (couple_hbm, couple),
+            ]
+        )
+    ]
+    for load in early + loads:
         load.start()
 
     def exists(q):
@@ -320,6 +339,8 @@
             total = total + ar2[i, d]
         return total
 
+    for load in early:
+        load.wait()
     for c in range(ROWS):
         cell[c : c + 1, :] = send[:, c * 128 : (c + 1) * 128]
 
@@ -839,7 +860,6 @@
     n_gx, n_gy = lax.axis_size("gx"), lax.axis_size("gy")
     vmem = pl.BlockSpec(memory_space=pltpu.VMEM)
     anywhere = pl.BlockSpec(memory_space=pl.ANY)
-    smem = pl.BlockSpec(memory_space=pltpu.SMEM)
     dma = pltpu.SemaphoreType.DMA
     scratch = [
         pltpu.VMEM((6, 9, CX, CY, CZ), F32),
@@ -872,7 +892,13 @@
         pltpu.VMEM((2, 2 * n_gy, 1, 128), F32),
         pltpu.VMEM((2, n_gx // 2, 1, 128), F32),
         pltpu.VMEM((8, 128), F32),
-        dma((5,)),
+        pltpu.VMEM((3, CX, CY, CZ), F32),
+        pltpu.VMEM((9, CX, CY, CZ), F32),
+        pltpu.VMEM((1, 3200), I32),
+        pltpu.VMEM((WELLS, MAXSEG), I32),
+        pltpu.SMEM((WELLS,), I32),
+        pltpu.VMEM((9, WELLS, NCHUNK), F32),
+        dma((11,)),
         dma((2, 9)),
         dma((2, 9)),
         dma((2, 9)),
@@ -892,7 +918,7 @@
             jax.ShapeDtypeStruct((2, 3, CX, CY, CZ), F32),
             jax.ShapeDtypeStruct((1, 128), F32),
         ),
-        in_specs=[vmem, vmem, anywhere, anywhere, vmem, vmem, smem, anywhere, vmem],
+        in_specs=[anywhere] * 9,
         out_specs=(anywhere, anywhere, vmem),
         scratch_shapes=scratch,
         compiler_params=pltpu.CompilerParams(collective_id=0, has_side_effects=True),

time: 59.4 us -> 58.3 us (0.981)
  Pallas kernels: 58.6 us -> 57.6 us
    pallas_call x1, Pallas kernels: 56.6 us -> 55.5 us  [body(): pl.pallas_call(functools.partial(kernel, n_gx, n_gy), out_shape=(jax.Shap...]
where the time goes in v5:
time: 58.3 us; the launch traced here: 58.2 us
  Pallas kernels  57.6 us (99%)
  between operations  0.64 us (1%)
    pallas_call x1, Pallas kernels, body(): pl.pallas_call(functools.partial(kernel, n_gx, n_gy), out_shape=(jax.Shap...  55.5 us
    pallas_call x1, Pallas kernels, body(): pl.pallas_call(combine, out_shape=(shape, shape), in_specs=[vmem] * 4, ou...  2.06 us

profile of v5, /device:TPU:0, one launch (start us, length us, event | category | flops | bytes accessed | tf_op | source)
XLA Modules:
  0.0 58.2 jit_solution(15721597083630863254)
XLA Ops:
  0.6 55.5 %gmres.1 = (f32[2,4,3,16,256]{4,3,2,1,0:T(8,128)}, f32[2,3,4,16,256]{4,3,2,1,0:T(8,128)}, f32[1,128]{1,0:T(1,128)}) custom-call(f32[3,4,16,256]{3,2,1,0:T(8,128)} %rhs.1, f32[9,4,16,256]{3,2,1,0:T(8,128)} %diag_hbm.1, f32[6,9,4,16,256]{4,3,2,1,0:T(8,128)} %off_hbm.1, f32[9,4,16,256]{3,2,1,0:T(8,128)} %cinv_hbm.1, s32[1,3200]{1,0:T(1,128)} %send_hbm.1, ...), custom_call_target="tpu_custom_call" | custom-call | tf_op jit(solution)/shard_map/gmres/pallas_call | solution.py:914
  56.1 2.1 %combine.1 = (f32[3,4,16,256]{3,2,1,0:T(8,128)}, f32[3,4,16,256]{3,2,1,0:T(8,128)}) custom-call(f32[3,4,16,256]{3,2,1,0:T(8,128)} %rhs.1, f32[2,4,3,16,256]{4,3,2,1,0:T(8,128)} %get-tuple-element.5.z, f32[2,3,4,16,256]{4,3,2,1,0:T(8,128)} %get-tuple-element.6.w, f32[1,128]{1,0:T(1,128)} %get-tuple-element.7.weights), custom_call_target="tpu_custom_call" | custom-call | tf_op jit(solution)/shard_map/combine/pallas_call | solution.py:938
